TPU v7x, 256 devices: a whole 4x4x8 slice. The times are simulated.
256 devices in a mesh: dp: 16 (over y, x), expert: 16 (over z, core).
Axes of the slice: x: 4, y: 4, z: 8, core: 2. Of those that a mesh axis runs over, the one named last changes fastest.
Arguments:
- tokens: bfloat16 [16384, 2048], P(('dp', 'expert')), may hold values from -6 to 6
- expert_ids: int32 [16384, 8], P(('dp', 'expert')), may hold values from 0 to 127, all different within a row; in each aligned block of 32 rows (0 to 31, 32 to 63, ...) at most 3 rows name the same one
- gate_fixed: int32 [16384, 8], P(('dp', 'expert')), may hold values from 1 to 65535
- w_gate: bfloat16 [256, 2048, 384], P(('dp', 'expert')), may hold values from -0.125 to 0.125
- w_up: bfloat16 [256, 2048, 384], P(('dp', 'expert')), may hold values from -0.125 to 0.125
- w_down: bfloat16 [256, 384, 2048], P(('dp', 'expert')), may hold values from -0.21875 to 0.21875
Outputs:
- mixed: float32 [16384, 2048], P(('dp', 'expert'))
Inputs may be any that keep to these rules, and one draw needn't show every extreme that they name: `expert_ids`: each row names 8 different experts. In each aligned block of 32 rows (the first or the second half of one device's rows) no expert is named by more than 3 rows, a bound that some block reaches.
All inputs are finite; a program needn't handle non-finite values.
Results may differ from a plain program's by a relative error of at most 0.0041.
Values may be sent and summed in bfloat16 or wider, within the bound.
No kernel may reach another device: no remote copies, remote signals or barrier semaphores. Data moves between devices by JAX's collectives and lax.ppermute only.
A program may use at most 64 MiB of HBM per device.

v0:
```python
import jax
import jax.numpy as jnp
from jax import lax
from jax.sharding import PartitionSpec as P


def partner(x, axis, stride):
    return lax.ppermute(x, axis, [(i, i ^ 1 << stride) for i in range(lax.axis_size(axis))])


def per_device(tokens, expert_ids, gate_fixed, w_gate, w_up, w_down):
    dp_count = lax.axis_size("dp")
    col_count = lax.axis_size("expert")
    pair_count = col_count // 2
    dev_count = dp_count * col_count
    expert_count = dev_count // 2
    token_count, width = tokens.shape
    choice_count = expert_ids.shape[1]
    capacity = 3 * token_count * choice_count // (4 * expert_count)
    half_rows = token_count // 2
    other_gate, other_up, other_down = partner((w_gate[0], w_up[0], w_down[0]), "expert", 0)
    gate_full = jnp.concatenate([w_gate[0], other_gate], axis=1)
    up_full = jnp.concatenate([w_up[0], other_up], axis=1)
    down_full = jnp.concatenate([w_down[0], other_down], axis=0)
    gates = gate_fixed.astype(jnp.float32)
    mix_weight = gates / jnp.sum(gates, axis=1, keepdims=True)
    flat_ids = expert_ids.reshape(-1)
    choice_pos = jnp.arange(token_count * choice_count, dtype=jnp.int32)
    half_index = choice_pos // choice_count // half_rows
    onehot = (flat_ids[:, None] == jnp.arange(expert_count, dtype=jnp.int32)[None, :]).astype(
        jnp.int32
    )
    onehot = onehot.reshape(2, half_rows * choice_count, expert_count)
    earlier = jnp.cumsum(onehot, axis=1) - onehot
    slot_index = jnp.sum(earlier * onehot, axis=2).reshape(-1)
    dest_dp = flat_ids // pair_count
    dest_col = 2 * (flat_ids % pair_count) + half_index
    target = (dest_dp * col_count + dest_col) * capacity + slot_index
    repeated = jnp.repeat(tokens, choice_count, axis=0)
    outgoing = jnp.zeros((dev_count * capacity, width), jnp.bfloat16).at[target].set(repeated)
    outgoing = outgoing.reshape(dp_count, col_count, capacity, width)
    first_section = lax.all_to_all(outgoing, "dp", split_axis=0, concat_axis=0, tiled=True)
    arrived = lax.all_to_all(first_section, "expert", split_axis=1, concat_axis=1, tiled=True)
    shape_in = arrived.shape
    token_rows = arrived.reshape(-1, width)
    gate_part = jnp.dot(token_rows, gate_full, preferred_element_type=jnp.float32)
    up_part = jnp.dot(token_rows, up_full, preferred_element_type=jnp.float32)
    hidden = (jax.nn.silu(gate_part) * up_part).astype(jnp.bfloat16)
    expert_out = jnp.dot(hidden, down_full, preferred_element_type=jnp.float32).astype(jnp.bfloat16)
    returned = lax.all_to_all(
        expert_out.reshape(shape_in), "expert", split_axis=1, concat_axis=1, tiled=True
    )
    home = lax.all_to_all(returned, "dp", split_axis=0, concat_axis=0, tiled=True)
    home_flat = home.reshape(dev_count * capacity, width)
    picked = home_flat[target].reshape(token_count, choice_count, width)
    mixed = jnp.sum(picked.astype(jnp.float32) * mix_weight[:, :, None], axis=1)
    return mixed


def solution(mesh):
    placed = (
        P(("dp", "expert"), None),
        P(("dp", "expert"), None),
        P(("dp", "expert"), None),
        P(("dp", "expert"), None, None),
        P(("dp", "expert"), None, None),
        P(("dp", "expert"), None, None),
    )
    return jax.shard_map(
        per_device, mesh=mesh, in_specs=placed, out_specs=P(("dp", "expert"), None), check_vma=False
    )
```

profile of v0, /device:TPU:96, one launch (start us, length us, event | category | flops | bytes accessed | tf_op | source)
XLA Modules:
  0.0 331.0 jit_solution(7348025419594827379)
XLA Ops:
  0.0 0.8 copy.14
  1.2 0.4 fusion.17
  2.2 4.6 %scatter_custom_fusion = bf16[768,2048]{1,0:T(8,128)(2,1)S(1)} fusion(s32[512]{0:T(512)S(1)} %bitcast.27, bf16[]{:T(256)} %constant.54.clone.1, bf16[64,2048]{1,0:T(8,128)(2,1)S(1)} %copy-done), kind=kCustom, calls=%fused_computation.17 | custom fusion | bytes 3407874 | tf_op jit(solution)/shard_map/scatter | solution.py:40
  6.8 4.4 %reshape.259 = bf16[16,16,3,2048]{3,2,1,0:T(4,128)(2,1)} reshape(bf16[768,2048]{1,0:T(8,128)(2,1)S(1)} %scatter_custom_fusion) | data formatting | bytes 6291456 | tf_op jit(solution)/shard_map/reshape | solution.py:41
  11.2 4.7 %copy.19 = bf16[16,16,3,2048]{3,1,2,0:T(8,128)(2,1)S(1)} copy(bf16[16,16,3,2048]{3,2,1,0:T(4,128)(2,1)} %reshape.259) | data formatting | bytes 6291456 | tf_op jit(solution)/shard_map/reshape | solution.py:41
  15.9 46.5 %all_to_all.20 = bf16[16,16,3,2048]{3,1,2,0:T(8,128)(2,1)S(1)} all-to-all(bf16[16,16,3,2048]{3,1,2,0:T(8,128)(2,1)S(1)} %copy.19), channel_id=1, replica_groups=mesh['dp'=16,'expert'=16] {'dp'}, dimensions={0} | all-to-all | bytes 6291456 | tf_op jit(solution)/shard_map/all_to_all | solution.py:42
  62.4 3.4 %copy.20 = bf16[16,16,3,2048]{3,0,2,1:T(8,128)(2,1)} copy(bf16[16,16,3,2048]{3,1,2,0:T(8,128)(2,1)S(1)} %all_to_all.20) | data formatting | bytes 6291456 | tf_op jit(solution)/shard_map/all_to_all | solution.py:42
  65.8 7.7 %all-to-all-start.1 = ((bf16[16,16,3,2048]{3,0,2,1:T(8,128)(2,1)}), bf16[16,16,3,2048]{3,0,2,1:T(8,128)(2,1)S(1)}, u32[]{:S(2)}, u32[]{:S(2)}) async-start(bf16[16,16,3,2048]{3,0,2,1:T(8,128)(2,1)} %copy.20), calls=%async_computation.1 | async-start | bytes 6291456 | tf_op jit(solution)/shard_map/all_to_all | solution.py:43
  74.1 70.5 %all-to-all-done.1 = bf16[16,16,3,2048]{3,0,2,1:T(8,128)(2,1)S(1)} async-done(((bf16[16,16,3,2048]{3,0,2,1:T(8,128)(2,1)}), bf16[16,16,3,2048]{3,0,2,1:T(8,128)(2,1)S(1)}, u32[]{:S(2)}, u32[]{:S(2)}) %all-to-all-start.1) | async-done | bytes 3145760 | tf_op jit(solution)/shard_map/all_to_all | solution.py:43
  144.6 4.6 %copy.21 = bf16[16,16,3,2048]{3,2,1,0:T(4,128)(2,1)} copy(bf16[16,16,3,2048]{3,0,2,1:T(8,128)(2,1)S(1)} %all-to-all-done.1) | data formatting | bytes 6291456 | tf_op jit(solution)/shard_map/all_to_all | solution.py:43
  149.3 7.5 %reshape.260 = bf16[768,2048]{1,0:T(8,128)(2,1)S(1)} reshape(bf16[16,16,3,2048]{3,2,1,0:T(4,128)(2,1)} %copy.21) | data formatting | bytes 6291456 | tf_op jit(solution)/shard_map/reshape | solution.py:45
  156.8 4.6 %fusion.1 = f32[768,768]{1,0:T(8,128)S(1)} fusion(bf16[768,2048]{1,0:T(8,128)(2,1)S(1)} %reshape.260, bf16[2048,384]{1,0:T(8,128)(2,1)} %collective-permute-done, bf16[2048,384]{1,0:T(8,128)(2,1)} %bitcast.31), kind=kOutput, calls=%fused_computation.5 | convolution fusion | flops 2422210560 | bytes 8650752 | tf_op jit(solution)/shard_map/dot_general | solution.py:46
  161.4 4.1 %fusion.5 = f32[768,768]{1,0:T(8,128)S(1)} fusion(bf16[768,2048]{1,0:T(8,128)(2,1)S(1)} %reshape.260, bf16[2048,384]{1,0:T(8,128)(2,1)} %collective-permute-done.1, bf16[2048,384]{1,0:T(8,128)(2,1)S(1)} %bitcast.33), kind=kOutput, calls=%fused_computation.9 | convolution fusion | flops 2422210560 | bytes 8650752 | tf_op jit(solution)/shard_map/dot_general | solution.py:47
  165.6 4.1 %convolution_convert_fusion = bf16[768,2048]{1,0:T(8,128)(2,1)S(1)} fusion(bf16[384,2048]{1,0:T(8,128)(2,1)} %collective-permute-done.2, bf16[384,2048]{1,0:T(8,128)(2,1)S(1)} %bitcast.35, f32[768,768]{1,0:T(8,128)S(1)} %fusion.5, f32[768,768]{1,0:T(8,128)S(1)} %fusion.1), kind=kOutput, calls=%fused_computation.4 | convolution fusion | flops 2427322368 | bytes 11010048 | tf_op jit(solution)/shard_map/dot_general | solution.py:49
  169.7 4.4 %reshape.261 = bf16[16,16,3,2048]{3,2,1,0:T(4,128)(2,1)} reshape(bf16[768,2048]{1,0:T(8,128)(2,1)S(1)} %convolution_convert_fusion) | data formatting | bytes 6291456 | tf_op jit(solution)/shard_map/reshape | solution.py:51
  174.1 4.7 %copy.22 = bf16[16,16,3,2048]{3,0,2,1:T(8,128)(2,1)S(1)} copy(bf16[16,16,3,2048]{3,2,1,0:T(4,128)(2,1)} %reshape.261) | data formatting | bytes 6291456 | tf_op jit(solution)/shard_map/reshape | solution.py:51
  178.8 76.2 %all_to_all.21 = bf16[16,16,3,2048]{3,0,2,1:T(8,128)(2,1)S(1)} all-to-all(bf16[16,16,3,2048]{3,0,2,1:T(8,128)(2,1)S(1)} %copy.22), channel_id=1, replica_groups=mesh['dp'=16,'expert'=16] {'expert'}, dimensions={1} | all-to-all | bytes 6291456 | tf_op jit(solution)/shard_map/all_to_all | solution.py:50
  255.0 3.4 %copy.23 = bf16[16,16,3,2048]{3,1,2,0:T(8,128)(2,1)} copy(bf16[16,16,3,2048]{3,0,2,1:T(8,128)(2,1)S(1)} %all_to_all.21) | data formatting | bytes 6291456 | tf_op jit(solution)/shard_map/all_to_all | solution.py:50
  258.4 4.1 %all-to-all-start.3 = ((bf16[16,16,3,2048]{3,1,2,0:T(8,128)(2,1)}), bf16[16,16,3,2048]{3,1,2,0:T(8,128)(2,1)S(1)}, u32[]{:S(2)}, u32[]{:S(2)}) async-start(bf16[16,16,3,2048]{3,1,2,0:T(8,128)(2,1)} %copy.23), calls=%async_computation.3 | async-start | bytes 6291456 | tf_op jit(solution)/shard_map/all_to_all | solution.py:53
  262.7 48.6 %all-to-all-done.3 = bf16[16,16,3,2048]{3,1,2,0:T(8,128)(2,1)S(1)} async-done(((bf16[16,16,3,2048]{3,1,2,0:T(8,128)(2,1)}), bf16[16,16,3,2048]{3,1,2,0:T(8,128)(2,1)S(1)}, u32[]{:S(2)}, u32[]{:S(2)}) %all-to-all-start.3) | async-done | bytes 3145760 | tf_op jit(solution)/shard_map/all_to_all | solution.py:53
  311.3 4.7 %copy.24 = bf16[16,16,3,2048]{3,2,1,0:T(4,128)(2,1)} copy(bf16[16,16,3,2048]{3,1,2,0:T(8,128)(2,1)S(1)} %all-to-all-done.3) | data formatting | bytes 6291456 | tf_op jit(solution)/shard_map/all_to_all | solution.py:53
  315.9 7.5 %reshape.262 = bf16[768,2048]{1,0:T(8,128)(2,1)S(1)} reshape(bf16[16,16,3,2048]{3,2,1,0:T(4,128)(2,1)} %copy.24) | data formatting | bytes 6291456 | tf_op jit(solution)/shard_map/reshape | solution.py:54
  323.5 3.3 %gather_fusion = bf16[512,2048]{1,0:T(8,128)(2,1)} fusion(bf16[768,2048]{1,0:T(8,128)(2,1)S(1)} %reshape.262, s32[1024]{0:T(1024)S(1)} %pad_clamp_fusion), kind=kCustom, calls=%fused_computation | custom fusion | bytes 4196352 | tf_op jit(solution)/shard_map/gather | solution.py:55
  326.8 4.2 %fusion = f32[64,2048]{1,0:T(8,128)} fusion(bf16[512,2048]{1,0:T(8,128)(2,1)} %gather_fusion, f32[64,8]{1,0:T(8,128)S(1)} %copy.25), kind=kLoop, calls=%fused_computation.3 | loop fusion | flops 3014656 | bytes 2623488 | tf_op jit(solution)/shard_map/reduce_sum | solution.py:56
  (32 shorter events, 1.7 us)
Async XLA Ops:
  0.0 2.2 copy-start
  65.8 78.9 %all-to-all-start.1 = ((bf16[16,16,3,2048]{3,0,2,1:T(8,128)(2,1)}), bf16[16,16,3,2048]{3,0,2,1:T(8,128)(2,1)S(1)}, u32[]{:S(2)}, u32[]{:S(2)}) async-start(bf16[16,16,3,2048]{3,0,2,1:T(8,128)(2,1)} %copy.20), calls=%async_computation.1 | async-start | bytes 6291456 | tf_op jit(solution)/shard_map/all_to_all | solution.py:43
  73.5 83.3 %collective-permute-start = (bf16[2048,384]{1,0:T(8,128)(2,1)}, bf16[2048,384]{1,0:T(8,128)(2,1)}, u32[]{:S(2)}, u32[]{:S(2)}) collective-permute-start(bf16[2048,384]{1,0:T(8,128)(2,1)} %bitcast.30), channel_id=1, source_target_pairs={{0,1},{1,0},{2,3},{3,2},{4,5},{5,4},{6,7},{7,6},{8,9},{9,8},{10,11... | collective-permute-start | bytes 4718600 | tf_op jit(solution)/shard_map/ppermute | solution.py:8
  73.6 87.8 %collective-permute-start.1 = (bf16[2048,384]{1,0:T(8,128)(2,1)}, bf16[2048,384]{1,0:T(8,128)(2,1)}, u32[]{:S(2)}, u32[]{:S(2)}) collective-permute-start(bf16[2048,384]{1,0:T(8,128)(2,1)} %bitcast.32), channel_id=1, source_target_pairs={{0,1},{1,0},{2,3},{3,2},{4,5},{5,4},{6,7},{7,6},{8,9},{9,8},{10,11... | collective-permute-start | bytes 4718600 | tf_op jit(solution)/shard_map/ppermute | solution.py:8
  74.0 91.6 %collective-permute-start.2 = (bf16[384,2048]{1,0:T(8,128)(2,1)}, bf16[384,2048]{1,0:T(8,128)(2,1)}, u32[]{:S(2)}, u32[]{:S(2)}) collective-permute-start(bf16[384,2048]{1,0:T(8,128)(2,1)} %bitcast.34), channel_id=1, source_target_pairs={{0,1},{1,0},{2,3},{3,2},{4,5},{5,4},{6,7},{7,6},{8,9},{9,8},{10,11... | collective-permute-start | bytes 4718600 | tf_op jit(solution)/shard_map/ppermute | solution.py:8
  156.8 4.6 %copy-start.3 = (bf16[1,2048,384]{2,1,0:T(8,128)(2,1)S(1)}, bf16[1,2048,384]{2,1,0:T(8,128)(2,1)}, u32[]{:S(2)}) copy-start(bf16[1,2048,384]{2,1,0:T(8,128)(2,1)} %param.10) | copy-start | bytes 4718596
  161.4 4.2 %copy-start.4 = (bf16[1,384,2048]{2,1,0:T(8,128)(2,1)S(1)}, bf16[1,384,2048]{2,1,0:T(8,128)(2,1)}, u32[]{:S(2)}) copy-start(bf16[1,384,2048]{2,1,0:T(8,128)(2,1)} %param.11) | copy-start | bytes 4718596
  258.4 4.1 %copy-start.2 = (s32[64,8]{0,1:T(8,128)S(1)}, s32[64,8]{0,1:T(8,128)}, u32[]{:S(2)}) copy-start(s32[64,8]{0,1:T(8,128)} %param.8) | copy-start | bytes 6148
  258.4 52.8 %all-to-all-start.3 = ((bf16[16,16,3,2048]{3,1,2,0:T(8,128)(2,1)}), bf16[16,16,3,2048]{3,1,2,0:T(8,128)(2,1)S(1)}, u32[]{:S(2)}, u32[]{:S(2)}) async-start(bf16[16,16,3,2048]{3,1,2,0:T(8,128)(2,1)} %copy.23), calls=%async_computation.3 | async-start | bytes 6291456 | tf_op jit(solution)/shard_map/all_to_all | solution.py:53
  323.5 7.6 %copy-start.1 = (bf16[64,2048]{1,0:T(8,128)(2,1)S(1)}, bf16[64,2048]{1,0:T(8,128)(2,1)}, u32[]{:S(2)}) copy-start(bf16[64,2048]{1,0:T(8,128)(2,1)} %param.6) | copy-start | bytes 786436
where the time goes:
time: 336 us; the launch traced here: 331 us
  blocking collectives  123 us (37%)
  waiting for transfers between devices  119 us (35%)
  local copies, waits for them, and re-layouts  58.7 us (17%)
  matrix products  12.8 us (4%)
  starting transfers between devices  12.5 us (4%)
  other arithmetic  5.1 us (2%)
    all_to_all x1, blocking collectives, per_device(): lax.all_to_all(expert_out.reshape(shape_in), 'expert', split_axis=1, conc...  76.2 us
    all_to_all x1, waiting for transfers between devices, per_device(): lax.all_to_all(first_section, 'expert', split_axis=1, concat_axis=1, tile...  70.5 us
    all_to_all x1, waiting for transfers between devices, per_device(): lax.all_to_all(returned, 'dp', split_axis=0, concat_axis=0, tiled=True)  48.6 us
    all_to_all x1, blocking collectives, per_device(): lax.all_to_all(outgoing, 'dp', split_axis=0, concat_axis=0, tiled=True)  46.5 us
    reshape x2, local copies, waits for them, and re-layouts, per_device(): outgoing = outgoing.reshape(dp_count, col_count, capacity, width)  9.13 us
    reshape x2, local copies, waits for them, and re-layouts, per_device(): expert_out.reshape(shape_in)  9.13 us
    all_to_all x1, starting transfers between devices, per_device(): lax.all_to_all(first_section, 'expert', split_axis=1, concat_axis=1, tile...  7.68 us
    reshape x1, local copies, waits for them, and re-layouts, per_device(): token_rows = arrived.reshape(-1, width)  7.51 us
  transfers between devices with their start and end apart: 5, of which 2 were waited for; matrix products, arithmetic and copies ran while one was open for 6% of the time, Pallas kernels for 0%

commit v1 on v0

v1 whole, which is shorter than its diff:
```python
import functools

import jax
import jax.numpy as jnp
from jax import lax
from jax.experimental import pallas as pl
from jax.experimental.pallas import tpu as pltpu
from jax.sharding import PartitionSpec as P

F32 = jnp.float32
BF16 = jnp.bfloat16
EXTRA = 128
VMEM = pl.BlockSpec(memory_space=pltpu.VMEM)
SMEM = pl.BlockSpec(memory_space=pltpu.SMEM)
PARAMS = pltpu.CompilerParams(vmem_limit_bytes=56 << 20)


def slot_of(index, slots):
    group = jnp.zeros_like(index)
    for d in range(1, 16):
        group = group + (index >= d * slots).astype(jnp.int32)
    return group, index - group * slots


def dispatch_kernel(slots, planes, z_ref, x_ref, out_ref):
    tokens = x_ref.shape[0]
    width = out_ref.shape[1]
    groups = out_ref.shape[0] // slots
    extra = x_ref[:, width:].astype(F32).T
    dest = planes * lax.broadcasted_iota(jnp.int32, (groups, 1), 0) + z_ref[0]
    dest = dest.astype(F32)
    match = jnp.zeros((groups, tokens), F32)
    for k in range(8):
        match = match + (extra[k : k + 1, :] == dest).astype(F32)
    upper = lax.broadcasted_iota(jnp.int32, (tokens, tokens), 0) <= lax.broadcasted_iota(
        jnp.int32, (tokens, tokens), 1
    )
    upper = upper.astype(F32).astype(BF16)
    order = jnp.dot(match.astype(BF16), upper, preferred_element_type=F32) * match
    row = lax.broadcasted_iota(jnp.int32, (groups * slots, 1), 0)
    group, place = slot_of(row, slots)
    spread = (group == lax.broadcasted_iota(jnp.int32, (1, groups), 1)).astype(F32).astype(BF16)
    wanted = jnp.dot(spread, order.astype(BF16), preferred_element_type=F32)
    pick = (wanted == (place + 1).astype(F32)).astype(F32).astype(BF16)
    out_ref[...] = jnp.dot(pick, x_ref[:, :width], preferred_element_type=F32).astype(BF16)


def expert_kernel(x_ref, g0, g1, u0, u1, d0, d1, out_ref):
    rows = x_ref.shape[0]
    step = 256
    for r in range(0, rows, step):
        x = x_ref[r : r + step, :]
        total = None
        for g_ref, u_ref, d_ref in ((g0, u0, d0), (g1, u1, d1)):
            gate = jnp.dot(x, g_ref[...], preferred_element_type=F32)
            up = jnp.dot(x, u_ref[...], preferred_element_type=F32)
            hidden = (gate / (1.0 + jnp.exp(-gate)) * up).astype(BF16)
            part = jnp.dot(hidden, d_ref[...], preferred_element_type=F32)
            total = part if total is None else total + part
        out_ref[r : r + step, :] = total.astype(BF16)


def combine_kernel(slots, planes, z_ref, extra_ref, home_ref, out_ref):
    tokens = extra_ref.shape[0]
    groups = home_ref.shape[0] // slots
    extra = extra_ref[...].astype(F32)
    gates = extra[:, 8:16] * 256.0 + extra[:, 16:24]
    mix = gates / jnp.sum(gates, axis=1, keepdims=True)
    dest = planes * lax.broadcasted_iota(jnp.int32, (1, EXTRA), 1) + z_ref[0]
    dest = dest.astype(F32)
    match = jnp.zeros((tokens, EXTRA), F32)
    weight = jnp.zeros((tokens, EXTRA), F32)
    for k in range(8):
        same = extra[:, k : k + 1] == dest
        match = match + same.astype(F32)
        weight = weight + jnp.where(same, mix[:, k : k + 1], 0.0)
    lower = lax.broadcasted_iota(jnp.int32, (tokens, tokens), 1) <= lax.broadcasted_iota(
        jnp.int32, (tokens, tokens), 0
    )
    lower = lower.astype(F32).astype(BF16)
    order = jnp.dot(lower, match.astype(BF16), preferred_element_type=F32) * match
    column = lax.broadcasted_iota(jnp.int32, (1, groups * slots), 1)
    group, place = slot_of(column, slots)
    spread = (group == lax.broadcasted_iota(jnp.int32, (EXTRA, 1), 0)).astype(F32).astype(BF16)
    wanted = jnp.dot(order.astype(BF16), spread, preferred_element_type=F32)
    here = wanted == (place + 1).astype(F32)
    high = weight.astype(BF16)
    low = (weight - high.astype(F32)).astype(BF16)
    home = home_ref[...]
    total = None
    for piece in (high, low):
        wide = jnp.dot(piece, spread, preferred_element_type=F32)
        wide = jnp.where(here, wide, 0.0).astype(BF16)
        part = jnp.dot(wide, home, preferred_element_type=F32)
        total = part if total is None else total + part
    out_ref[...] = total


def per_device(tokens, expert_ids, gate_fixed, w_gate, w_up, w_down):
    col_count = lax.axis_size("expert")
    dp_count = lax.axis_size("dp")
    planes = col_count // 2
    rows, width = tokens.shape
    block = 3 * rows // 32
    slots = block * planes // 2
    plane = (lax.axis_index("expert") // 2).astype(jnp.int32).reshape(1)

    def along_z(x, by):
        return lax.ppermute(
            x, "expert", [(i, (i + 2 * by) % col_count) for i in range(col_count)]
        )

    def partner(x):
        return lax.ppermute(x, "expert", [(i, i ^ 1) for i in range(col_count)])

    packed = jnp.concatenate(
        [expert_ids, gate_fixed // 256, gate_fixed % 256, jnp.zeros((rows, EXTRA - 24), jnp.int32)],
        axis=1,
    ).astype(BF16)
    mine = jnp.concatenate([tokens, packed], axis=1)
    half = planes // 2
    up = down = mine
    shards = [mine]
    for step in range(half):
        up = along_z(up, 1)
        shards.append(up)
        if step < half - 1:
            down = along_z(down, -1)
            shards.append(down)
    gathered = jnp.concatenate(shards, axis=0)
    weights = []
    for w in (w_gate[0], w_up[0], w_down[0]):
        weights += [w, partner(w)]

    slots = 3 * planes * rows // 32
    outgoing = pl.pallas_call(
        functools.partial(dispatch_kernel, slots, planes),
        out_shape=jax.ShapeDtypeStruct((dp_count * slots, width), BF16),
        in_specs=[SMEM, VMEM],
        out_specs=VMEM,
        compiler_params=PARAMS,
        name="dispatch",
    )(plane, gathered)
    arrived = lax.all_to_all(outgoing, "dp", split_axis=0, concat_axis=0, tiled=True)
    expert_out = pl.pallas_call(
        expert_kernel,
        out_shape=jax.ShapeDtypeStruct(arrived.shape, BF16),
        in_specs=[VMEM] * 7,
        out_specs=VMEM,
        compiler_params=PARAMS,
        name="expert",
    )(arrived, *weights)
    home = lax.all_to_all(expert_out, "dp", split_axis=0, concat_axis=0, tiled=True)
    partial = pl.pallas_call(
        functools.partial(combine_kernel, slots, planes),
        out_shape=jax.ShapeDtypeStruct((planes * rows, width), F32),
        in_specs=[SMEM, VMEM, VMEM],
        out_specs=VMEM,
        compiler_params=PARAMS,
        name="combine",
    )(plane, gathered[:, width:], home)

    part = [partial[i * rows : (i + 1) * rows] for i in range(planes)]
    from_low = [part[2 * i - 1] for i in range(1, half + 1)]
    from_high = [part[2 * i] for i in range(1, half)]
    down = from_low[half - 1].astype(BF16)
    up = from_high[half - 2].astype(BF16)
    for step in range(half):
        down = along_z(down, -1)
        if step < half - 1:
            down = (down.astype(F32) + from_low[half - 2 - step]).astype(BF16)
            up = along_z(up, 1)
            if step < half - 2:
                up = (up.astype(F32) + from_high[half - 3 - step]).astype(BF16)
    return part[0] + up.astype(F32) + down.astype(F32)


def solution(mesh):
    rows = P(("dp", "expert"), None)
    panels = P(("dp", "expert"), None, None)
    return jax.shard_map(
        per_device,
        mesh=mesh,
        in_specs=(rows, rows, rows, panels, panels, panels),
        out_specs=rows,
        check_vma=False,
    )
```

time: 336 us -> 211 us (0.63)
  blocking collectives: 123 us -> 0 us
  local copies, waits for them, and re-layouts: 58.7 us -> 9.66 us
  Pallas kernels: 0 us -> 32 us
  starting transfers between devices: 12.5 us -> 34.9 us
  matrix products: 12.8 us -> 0 us
  waiting for transfers between devices: 119 us -> 126 us
    all_to_all x2 -> x0, blocking collectives: 123 us -> none  [the longest x1 76.2 us: per_device(): lax.all_to_all(expert_out.reshape(shape_in), 'expert', split_axis=1, conc...]
    ppermute x3 -> x17, waiting for transfers between devices: 0.01 us -> 52.8 us  [the longest x14 45.3 us: along_z(): lax.ppermute(x, 'expert', [(i, (i + 2 * by) % col_count) for i in range(c...]
    all_to_all x2, waiting for transfers between devices: 119 us -> 73.1 us  [the longest x1 43.7 us: per_device(): lax.all_to_all(expert_out, 'dp', split_axis=0, concat_axis=0, tiled=True)]
    reshape x7 -> x0, local copies, waits for them, and re-layouts: 33.4 us -> none  [the longest x2 9.13 us: per_device(): outgoing = outgoing.reshape(dp_count, col_count, capacity, width)]
    pallas_call x0 -> x3, Pallas kernels: none -> 32 us  [the longest x1 16.5 us: per_device(): pl.pallas_call(expert_kernel, out_shape=jax.ShapeDtypeStruct(arrived.shap...]
    ppermute x3 -> x17, starting transfers between devices: 0.66 us -> 24 us  [the longest x14 23.3 us: along_z(): lax.ppermute(x, 'expert', [(i, (i + 2 * by) % col_count) for i in range(c...]
    all_to_all x4 -> x0, local copies, waits for them, and re-layouts: 16.1 us -> none  [the longest x1 4.69 us: per_device(): lax.all_to_all(returned, 'dp', split_axis=0, concat_axis=0, tiled=True)]
    dot_general x3 -> x0, matrix products: 12.8 us -> none  [the longest x1 4.59 us: per_device(): jnp.dot(token_rows, gate_full, preferred_element_type=jnp.float32)]
  transfers between devices with their start and end apart: 5 -> 19, of which waited for: 2 -> 13; matrix products, arithmetic and copies ran while one was open for 6% -> 1% of each run, Pallas kernels for 0% -> 0%
where the time goes in v1:
time: 211 us; the launch traced here: 207 us
  waiting for transfers between devices  126 us (60%)
  starting transfers between devices  34.9 us (17%)
  Pallas kernels  32 us (15%)
  local copies, waits for them, and re-layouts  9.66 us (5%)
  other arithmetic  4.54 us (2%)
    ppermute x14, waiting for transfers between devices, along_z(): lax.ppermute(x, 'expert', [(i, (i + 2 * by) % col_count) for i in range(c...  45.3 us
    all_to_all x1, waiting for transfers between devices, per_device(): lax.all_to_all(expert_out, 'dp', split_axis=0, concat_axis=0, tiled=True)  43.7 us
    all_to_all x1, waiting for transfers between devices, per_device(): lax.all_to_all(outgoing, 'dp', split_axis=0, concat_axis=0, tiled=True)  29.3 us
    ppermute x14, starting transfers between devices, along_z(): lax.ppermute(x, 'expert', [(i, (i + 2 * by) % col_count) for i in range(c...  23.3 us
    pallas_call x1, Pallas kernels, per_device(): pl.pallas_call(expert_kernel, out_shape=jax.ShapeDtypeStruct(arrived.shap...  16.5 us
    pallas_call x1, Pallas kernels, per_device(): pl.pallas_call(functools.partial(combine_kernel, slots, planes), out_shap...  10.1 us
    ppermute x3, waiting for transfers between devices, partner(): return lax.ppermute(x, 'expert', [(i, i ^ 1) for i in range(col_count)])  7.51 us
    all_to_all x1, starting transfers between devices, per_device(): lax.all_to_all(outgoing, 'dp', split_axis=0, concat_axis=0, tiled=True)  7.03 us
  transfers between devices with their start and end apart: 19, of which 13 were waited for; matrix products, arithmetic and copies ran while one was open for 1% of the time, Pallas kernels for 0%

profile of v1, /device:TPU:96, one launch (start us, length us, event | category | flops | bytes accessed | tf_op | source)
XLA Modules:
  0.0 207.3 jit_solution(3767835387106690202)
XLA Ops:
  2.7 3.2 %collective-permute-start = (bf16[64,2176]{1,0:T(8,128)(2,1)S(1)}, bf16[64,2176]{1,0:T(8,128)(2,1)S(1)}, u32[]{:S(2)}, u32[]{:S(2)}) collective-permute-start(bf16[64,2176]{1,0:T(8,128)(2,1)S(1)} %concatenate.9), channel_id=1, source_target_pairs={{0,2},{1,3},{2,4},{3,5},{4,6},{5,7},{6,8},{7,9},{8,10},{9,11},{10,... | collective-permute-start | bytes 835592 | tf_op jit(solution)/shard_map/ppermute | solution.py:109
  5.9 5.9 %collective-permute-done = bf16[64,2176]{1,0:T(8,128)(2,1)S(1)} collective-permute-done((bf16[64,2176]{1,0:T(8,128)(2,1)S(1)}, bf16[64,2176]{1,0:T(8,128)(2,1)S(1)}, u32[]{:S(2)}, u32[]{:S(2)}) %collective-permute-start) | collective-permute-done | bytes 278560 | tf_op jit(solution)/shard_map/ppermute | solution.py:109
  11.8 3.7 %collective-permute-start.2 = (bf16[64,2176]{1,0:T(8,128)(2,1)S(1)}, bf16[64,2176]{1,0:T(8,128)(2,1)S(1)}, u32[]{:S(2)}, u32[]{:S(2)}) collective-permute-start(bf16[64,2176]{1,0:T(8,128)(2,1)S(1)} %collective-permute-done), channel_id=1, source_target_pairs={{0,2},{1,3},{2,4},{3,5},{4,6},{5,7},{6,8},{7,9},{8,10},{9,11},{10,... | collective-permute-start | bytes 835592 | tf_op jit(solution)/shard_map/ppermute | solution.py:109
  15.6 4.9 %collective-permute-done.2 = bf16[64,2176]{1,0:T(8,128)(2,1)S(1)} collective-permute-done((bf16[64,2176]{1,0:T(8,128)(2,1)S(1)}, bf16[64,2176]{1,0:T(8,128)(2,1)S(1)}, u32[]{:S(2)}, u32[]{:S(2)}) %collective-permute-start.2) | collective-permute-done | bytes 278560 | tf_op jit(solution)/shard_map/ppermute | solution.py:109
  20.5 3.7 %collective-permute-start.4 = (bf16[64,2176]{1,0:T(8,128)(2,1)S(1)}, bf16[64,2176]{1,0:T(8,128)(2,1)S(1)}, u32[]{:S(2)}, u32[]{:S(2)}) collective-permute-start(bf16[64,2176]{1,0:T(8,128)(2,1)S(1)} %collective-permute-done.2), channel_id=1, source_target_pairs={{0,2},{1,3},{2,4},{3,5},{4,6},{5,7},{6,8},{7,9},{8,10},{9,11},{10,... | collective-permute-start | bytes 835592 | tf_op jit(solution)/shard_map/ppermute | solution.py:109
  24.4 4.0 %collective-permute-done.4 = bf16[64,2176]{1,0:T(8,128)(2,1)S(1)} collective-permute-done((bf16[64,2176]{1,0:T(8,128)(2,1)S(1)}, bf16[64,2176]{1,0:T(8,128)(2,1)S(1)}, u32[]{:S(2)}, u32[]{:S(2)}) %collective-permute-start.4) | collective-permute-done | bytes 278560 | tf_op jit(solution)/shard_map/ppermute | solution.py:109
  28.3 3.7 %collective-permute-start.6 = (bf16[64,2176]{1,0:T(8,128)(2,1)S(1)}, bf16[64,2176]{1,0:T(8,128)(2,1)S(1)}, u32[]{:S(2)}, u32[]{:S(2)}) collective-permute-start(bf16[64,2176]{1,0:T(8,128)(2,1)S(1)} %collective-permute-done.4), channel_id=1, source_target_pairs={{0,2},{1,3},{2,4},{3,5},{4,6},{5,7},{6,8},{7,9},{8,10},{9,11},{10,... | collective-permute-start | bytes 835592 | tf_op jit(solution)/shard_map/ppermute | solution.py:109
  32.1 4.0 %collective-permute-done.6 = bf16[64,2176]{1,0:T(8,128)(2,1)S(1)} collective-permute-done((bf16[64,2176]{1,0:T(8,128)(2,1)S(1)}, bf16[64,2176]{1,0:T(8,128)(2,1)S(1)}, u32[]{:S(2)}, u32[]{:S(2)}) %collective-permute-start.6) | collective-permute-done | bytes 278560 | tf_op jit(solution)/shard_map/ppermute | solution.py:109
  37.6 5.4 %dispatch.1 = bf16[768,2048]{1,0:T(8,128)(2,1)} custom-call(s32[1]{0:T(128)} %bitcast.z_ref, bf16[512,2176]{1,0:T(8,128)(2,1)} %copy-done.3), custom_call_target="tpu_custom_call" | custom-call | tf_op jit(solution)/shard_map/dispatch/pallas_call | solution.py:136
  43.0 7.0 %all-to-all-start = ((bf16[16,48,2048]{2,1,0:T(8,128)(2,1)}), bf16[16,48,2048]{2,1,0:T(8,128)(2,1)S(1)}, u32[]{:S(2)}, u32[]{:S(2)}) async-start(bf16[16,48,2048]{2,1,0:T(8,128)(2,1)} %bitcast.8), calls=%async_computation | async-start | bytes 6291456 | tf_op jit(solution)/shard_map/all_to_all | solution.py:144
  50.8 3.0 %collective-permute-done.7.g1 = bf16[2048,384]{1,0:T(8,128)(2,1)S(1)} collective-permute-done((bf16[2048,384]{1,0:T(8,128)(2,1)}, bf16[2048,384]{1,0:T(8,128)(2,1)S(1)}, u32[]{:S(2)}, u32[]{:S(2)}) %collective-permute-start.7) | collective-permute-done | bytes 1572896 | tf_op jit(solution)/shard_map/ppermute | solution.py:114
  53.8 4.5 %collective-permute-done.8.u1 = bf16[2048,384]{1,0:T(8,128)(2,1)S(1)} collective-permute-done((bf16[2048,384]{1,0:T(8,128)(2,1)}, bf16[2048,384]{1,0:T(8,128)(2,1)S(1)}, u32[]{:S(2)}, u32[]{:S(2)}) %collective-permute-start.8) | collective-permute-done | bytes 1572896 | tf_op jit(solution)/shard_map/ppermute | solution.py:114
  59.4 29.3 %all-to-all-done = bf16[16,48,2048]{2,1,0:T(8,128)(2,1)S(1)} async-done(((bf16[16,48,2048]{2,1,0:T(8,128)(2,1)}), bf16[16,48,2048]{2,1,0:T(8,128)(2,1)S(1)}, u32[]{:S(2)}, u32[]{:S(2)}) %all-to-all-start) | async-done | bytes 3145760 | tf_op jit(solution)/shard_map/all_to_all | solution.py:144
  90.4 16.5 %expert.1 = bf16[768,2048]{1,0:T(8,128)(2,1)} custom-call(bf16[768,2048]{1,0:T(8,128)(2,1)} %bitcast.10, bf16[2048,384]{1,0:T(8,128)(2,1)} %bitcast.13, bf16[2048,384]{1,0:T(8,128)(2,1)} %copy-done.4, bf16[2048,384]{1,0:T(8,128)(2,1)} %bitcast.15, bf16[2048,384]{1,0:T(8,128)(2,1)} %copy-done.5, bf16[384,2048]{1,0:T(8,128)(2,1)} %bitcast.17, ...), custom_call_target="tpu_custom_call" | custom-call | tf_op jit(solution)/shard_map/expert/pallas_call | solution.py:145
  106.9 4.0 %all-to-all-start.1 = ((bf16[16,48,2048]{2,1,0:T(8,128)(2,1)}), bf16[16,48,2048]{2,1,0:T(8,128)(2,1)S(1)}, u32[]{:S(2)}, u32[]{:S(2)}) async-start(bf16[16,48,2048]{2,1,0:T(8,128)(2,1)} %bitcast.11), calls=%async_computation.1 | async-start | bytes 6291456 | tf_op jit(solution)/shard_map/all_to_all | solution.py:153
  112.4 43.7 %all-to-all-done.1 = bf16[16,48,2048]{2,1,0:T(8,128)(2,1)S(1)} async-done(((bf16[16,48,2048]{2,1,0:T(8,128)(2,1)}), bf16[16,48,2048]{2,1,0:T(8,128)(2,1)S(1)}, u32[]{:S(2)}, u32[]{:S(2)}) %all-to-all-start.1) | async-done | bytes 3145760 | tf_op jit(solution)/shard_map/all_to_all | solution.py:153
  157.8 10.1 %combine.1 = f32[512,2048]{1,0:T(8,128)} custom-call(s32[1]{0:T(128)} %bitcast.z_ref, bf16[512,128]{1,0:T(8,128)(2,1)} %slice.38.extra_ref, bf16[768,2048]{1,0:T(8,128)(2,1)} %bitcast.9), custom_call_target="tpu_custom_call" | custom-call | tf_op jit(solution)/shard_map/combine/pallas_call | solution.py:154
  171.2 2.8 %collective-permute-start.10 = (bf16[64,2048]{1,0:T(8,128)(2,1)S(1)}, bf16[64,2048]{1,0:T(8,128)(2,1)S(1)}, u32[]{:S(2)}, u32[]{:S(2)}) collective-permute-start(bf16[64,2048]{1,0:T(8,128)(2,1)S(1)} %get-tuple-element.9), channel_id=1, source_target_pairs={{0,2},{1,3},{2,4},{3,5},{4,6},{5,7},{6,8},{7,9},{8,10},{9,11},{10,... | collective-permute-start | bytes 786440 | tf_op jit(solution)/shard_map/ppermute | solution.py:109
  174.0 4.3 %collective-permute-done.13 = bf16[64,2048]{1,0:T(8,128)(2,1)S(1)} collective-permute-done((bf16[64,2048]{1,0:T(8,128)(2,1)S(1)}, bf16[64,2048]{1,0:T(8,128)(2,1)S(1)}, u32[]{:S(2)}, u32[]{:S(2)}) %collective-permute-start.13) | collective-permute-done | bytes 262176 | tf_op jit(solution)/shard_map/ppermute | solution.py:109
  178.5 7.6 %collective-permute-done.14 = bf16[64,2048]{1,0:T(8,128)(2,1)S(1)} collective-permute-done((bf16[64,2048]{1,0:T(8,128)(2,1)S(1)}, bf16[64,2048]{1,0:T(8,128)(2,1)S(1)}, u32[]{:S(2)}, u32[]{:S(2)}) %collective-permute-start.14) | collective-permute-done | bytes 262176 | tf_op jit(solution)/shard_map/ppermute | solution.py:109
  188.3 5.0 %collective-permute-done.11 = bf16[64,2048]{1,0:T(8,128)(2,1)S(1)} collective-permute-done((bf16[64,2048]{1,0:T(8,128)(2,1)S(1)}, bf16[64,2048]{1,0:T(8,128)(2,1)S(1)}, u32[]{:S(2)}, u32[]{:S(2)}) %collective-permute-start.11) | collective-permute-done | bytes 262176 | tf_op jit(solution)/shard_map/ppermute | solution.py:109
  193.3 5.3 %collective-permute-done.15 = bf16[64,2048]{1,0:T(8,128)(2,1)S(1)} collective-permute-done((bf16[64,2048]{1,0:T(8,128)(2,1)S(1)}, bf16[64,2048]{1,0:T(8,128)(2,1)S(1)}, u32[]{:S(2)}, u32[]{:S(2)}) %collective-permute-start.15) | collective-permute-done | bytes 262176 | tf_op jit(solution)/shard_map/ppermute | solution.py:109
  198.8 3.2 %collective-permute-start.12 = (bf16[64,2048]{1,0:T(8,128)(2,1)S(1)}, bf16[64,2048]{1,0:T(8,128)(2,1)S(1)}, u32[]{:S(2)}, u32[]{:S(2)}) collective-permute-start(bf16[64,2048]{1,0:T(8,128)(2,1)S(1)} %get-tuple-element.5), channel_id=1, source_target_pairs={{0,2},{1,3},{2,4},{3,5},{4,6},{5,7},{6,8},{7,9},{8,10},{9,11},{10,... | collective-permute-start | bytes 786440 | tf_op jit(solution)/shard_map/ppermute | solution.py:109
  202.0 4.3 %collective-permute-done.16 = bf16[64,2048]{1,0:T(8,128)(2,1)S(1)} collective-permute-done((bf16[64,2048]{1,0:T(8,128)(2,1)S(1)}, bf16[64,2048]{1,0:T(8,128)(2,1)S(1)}, u32[]{:S(2)}, u32[]{:S(2)}) %collective-permute-start.16) | collective-permute-done | bytes 262176 | tf_op jit(solution)/shard_map/ppermute | solution.py:109
  (50 shorter events, 17.9 us)
Async XLA Ops:
  2.7 9.1 %collective-permute-start = (bf16[64,2176]{1,0:T(8,128)(2,1)S(1)}, bf16[64,2176]{1,0:T(8,128)(2,1)S(1)}, u32[]{:S(2)}, u32[]{:S(2)}) collective-permute-start(bf16[64,2176]{1,0:T(8,128)(2,1)S(1)} %concatenate.9), channel_id=1, source_target_pairs={{0,2},{1,3},{2,4},{3,5},{4,6},{5,7},{6,8},{7,9},{8,10},{9,11},{10,... | collective-permute-start | bytes 835592 | tf_op jit(solution)/shard_map/ppermute | solution.py:109
  5.9 9.6 %collective-permute-start.1 = (bf16[64,2176]{1,0:T(8,128)(2,1)S(1)}, bf16[64,2176]{1,0:T(8,128)(2,1)S(1)}, u32[]{:S(2)}, u32[]{:S(2)}) collective-permute-start(bf16[64,2176]{1,0:T(8,128)(2,1)S(1)} %concatenate.9), channel_id=1, source_target_pairs={{0,14},{1,15},{2,0},{3,1},{4,2},{5,3},{6,4},{7,5},{8,6},{9,7},{10,... | collective-permute-start | bytes 835592 | tf_op jit(solution)/shard_map/ppermute | solution.py:109
  11.8 8.7 %collective-permute-start.2 = (bf16[64,2176]{1,0:T(8,128)(2,1)S(1)}, bf16[64,2176]{1,0:T(8,128)(2,1)S(1)}, u32[]{:S(2)}, u32[]{:S(2)}) collective-permute-start(bf16[64,2176]{1,0:T(8,128)(2,1)S(1)} %collective-permute-done), channel_id=1, source_target_pairs={{0,2},{1,3},{2,4},{3,5},{4,6},{5,7},{6,8},{7,9},{8,10},{9,11},{10,... | collective-permute-start | bytes 835592 | tf_op jit(solution)/shard_map/ppermute | solution.py:109
  15.5 8.7 %collective-permute-start.3 = (bf16[64,2176]{1,0:T(8,128)(2,1)S(1)}, bf16[64,2176]{1,0:T(8,128)(2,1)S(1)}, u32[]{:S(2)}, u32[]{:S(2)}) collective-permute-start(bf16[64,2176]{1,0:T(8,128)(2,1)S(1)} %collective-permute-done.1), channel_id=1, source_target_pairs={{0,14},{1,15},{2,0},{3,1},{4,2},{5,3},{6,4},{7,5},{8,6},{9,7},{10,... | collective-permute-start | bytes 835592 | tf_op jit(solution)/shard_map/ppermute | solution.py:109
  20.5 7.8 %collective-permute-start.4 = (bf16[64,2176]{1,0:T(8,128)(2,1)S(1)}, bf16[64,2176]{1,0:T(8,128)(2,1)S(1)}, u32[]{:S(2)}, u32[]{:S(2)}) collective-permute-start(bf16[64,2176]{1,0:T(8,128)(2,1)S(1)} %collective-permute-done.2), channel_id=1, source_target_pairs={{0,2},{1,3},{2,4},{3,5},{4,6},{5,7},{6,8},{7,9},{8,10},{9,11},{10,... | collective-permute-start | bytes 835592 | tf_op jit(solution)/shard_map/ppermute | solution.py:109
  24.3 7.8 %collective-permute-start.5 = (bf16[64,2176]{1,0:T(8,128)(2,1)S(1)}, bf16[64,2176]{1,0:T(8,128)(2,1)S(1)}, u32[]{:S(2)}, u32[]{:S(2)}) collective-permute-start(bf16[64,2176]{1,0:T(8,128)(2,1)S(1)} %collective-permute-done.3), channel_id=1, source_target_pairs={{0,14},{1,15},{2,0},{3,1},{4,2},{5,3},{6,4},{7,5},{8,6},{9,7},{10,... | collective-permute-start | bytes 835592 | tf_op jit(solution)/shard_map/ppermute | solution.py:109
  28.3 7.8 %collective-permute-start.6 = (bf16[64,2176]{1,0:T(8,128)(2,1)S(1)}, bf16[64,2176]{1,0:T(8,128)(2,1)S(1)}, u32[]{:S(2)}, u32[]{:S(2)}) collective-permute-start(bf16[64,2176]{1,0:T(8,128)(2,1)S(1)} %collective-permute-done.4), channel_id=1, source_target_pairs={{0,2},{1,3},{2,4},{3,5},{4,6},{5,7},{6,8},{7,9},{8,10},{9,11},{10,... | collective-permute-start | bytes 835592 | tf_op jit(solution)/shard_map/ppermute | solution.py:109
  36.1 1.4 copy-start.3
  43.0 45.7 %all-to-all-start = ((bf16[16,48,2048]{2,1,0:T(8,128)(2,1)}), bf16[16,48,2048]{2,1,0:T(8,128)(2,1)S(1)}, u32[]{:S(2)}, u32[]{:S(2)}) async-start(bf16[16,48,2048]{2,1,0:T(8,128)(2,1)} %bitcast.8), calls=%async_computation | async-start | bytes 6291456 | tf_op jit(solution)/shard_map/all_to_all | solution.py:144
  50.1 3.7 %collective-permute-start.7 = (bf16[2048,384]{1,0:T(8,128)(2,1)}, bf16[2048,384]{1,0:T(8,128)(2,1)S(1)}, u32[]{:S(2)}, u32[]{:S(2)}) collective-permute-start(bf16[2048,384]{1,0:T(8,128)(2,1)} %bitcast.12), channel_id=1, source_target_pairs={{0,1},{1,0},{2,3},{3,2},{4,5},{5,4},{6,7},{7,6},{8,9},{9,8},{10,11... | collective-permute-start | bytes 4718600 | tf_op jit(solution)/shard_map/ppermute | solution.py:114
  50.2 8.1 %collective-permute-start.8 = (bf16[2048,384]{1,0:T(8,128)(2,1)}, bf16[2048,384]{1,0:T(8,128)(2,1)S(1)}, u32[]{:S(2)}, u32[]{:S(2)}) collective-permute-start(bf16[2048,384]{1,0:T(8,128)(2,1)} %bitcast.14), channel_id=1, source_target_pairs={{0,1},{1,0},{2,3},{3,2},{4,5},{5,4},{6,7},{7,6},{8,9},{9,8},{10,11... | collective-permute-start | bytes 4718600 | tf_op jit(solution)/shard_map/ppermute | solution.py:114
  50.6 8.8 %collective-permute-start.9 = (bf16[384,2048]{1,0:T(8,128)(2,1)}, bf16[384,2048]{1,0:T(8,128)(2,1)}, u32[]{:S(2)}, u32[]{:S(2)}) collective-permute-start(bf16[384,2048]{1,0:T(8,128)(2,1)} %bitcast.16), channel_id=1, source_target_pairs={{0,1},{1,0},{2,3},{3,2},{4,5},{5,4},{6,7},{7,6},{8,9},{9,8},{10,11... | collective-permute-start | bytes 4718600 | tf_op jit(solution)/shard_map/ppermute | solution.py:114
  53.8 4.5 %copy-start.4 = (bf16[2048,384]{1,0:T(8,128)(2,1)}, bf16[2048,384]{1,0:T(8,128)(2,1)S(1)}, u32[]{:S(2)}) copy-start(bf16[2048,384]{1,0:T(8,128)(2,1)S(1)} %collective-permute-done.7.g1) | copy-start | bytes 4718596
  88.7 1.7 copy-start.2
  106.9 49.3 %all-to-all-start.1 = ((bf16[16,48,2048]{2,1,0:T(8,128)(2,1)}), bf16[16,48,2048]{2,1,0:T(8,128)(2,1)S(1)}, u32[]{:S(2)}, u32[]{:S(2)}) async-start(bf16[16,48,2048]{2,1,0:T(8,128)(2,1)} %bitcast.11), calls=%async_computation.1 | async-start | bytes 6291456 | tf_op jit(solution)/shard_map/all_to_all | solution.py:153
  156.2 1.7 copy-start.1
  168.0 10.4 %copy-start = (f32[512,2048]{1,0:T(8,128)S(1)}, f32[512,2048]{1,0:T(8,128)}, u32[]{:S(2)}) copy-start(f32[512,2048]{1,0:T(8,128)} %combine.1) | copy-start | bytes 12582916
  170.7 7.7 %collective-permute-start.13 = (bf16[64,2048]{1,0:T(8,128)(2,1)S(1)}, bf16[64,2048]{1,0:T(8,128)(2,1)S(1)}, u32[]{:S(2)}, u32[]{:S(2)}) collective-permute-start(bf16[64,2048]{1,0:T(8,128)(2,1)S(1)} %get-tuple-element.10), channel_id=1, source_target_pairs={{0,14},{1,15},{2,0},{3,1},{4,2},{5,3},{6,4},{7,5},{8,6},{9,7},{10,... | collective-permute-start | bytes 786440 | tf_op jit(solution)/shard_map/ppermute | solution.py:109
  171.2 7.3 %collective-permute-start.10 = (bf16[64,2048]{1,0:T(8,128)(2,1)S(1)}, bf16[64,2048]{1,0:T(8,128)(2,1)S(1)}, u32[]{:S(2)}, u32[]{:S(2)}) collective-permute-start(bf16[64,2048]{1,0:T(8,128)(2,1)S(1)} %get-tuple-element.9), channel_id=1, source_target_pairs={{0,2},{1,3},{2,4},{3,5},{4,6},{5,7},{6,8},{7,9},{8,10},{9,11},{10,... | collective-permute-start | bytes 786440 | tf_op jit(solution)/shard_map/ppermute | solution.py:109
  178.4 7.7 %collective-permute-start.14 = (bf16[64,2048]{1,0:T(8,128)(2,1)S(1)}, bf16[64,2048]{1,0:T(8,128)(2,1)S(1)}, u32[]{:S(2)}, u32[]{:S(2)}) collective-permute-start(bf16[64,2048]{1,0:T(8,128)(2,1)S(1)} %fusion.2), channel_id=1, source_target_pairs={{0,14},{1,15},{2,0},{3,1},{4,2},{5,3},{6,4},{7,5},{8,6},{9,7},{10,... | collective-permute-start | bytes 786440 | tf_op jit(solution)/shard_map/ppermute | solution.py:109
  186.2 7.2 %collective-permute-start.11 = (bf16[64,2048]{1,0:T(8,128)(2,1)S(1)}, bf16[64,2048]{1,0:T(8,128)(2,1)S(1)}, u32[]{:S(2)}, u32[]{:S(2)}) collective-permute-start(bf16[64,2048]{1,0:T(8,128)(2,1)S(1)} %get-tuple-element.7), channel_id=1, source_target_pairs={{0,2},{1,3},{2,4},{3,5},{4,6},{5,7},{6,8},{7,9},{8,10},{9,11},{10,... | collective-permute-start | bytes 786440 | tf_op jit(solution)/shard_map/ppermute | solution.py:109
  188.3 10.3 %collective-permute-start.15 = (bf16[64,2048]{1,0:T(8,128)(2,1)S(1)}, bf16[64,2048]{1,0:T(8,128)(2,1)S(1)}, u32[]{:S(2)}, u32[]{:S(2)}) collective-permute-start(bf16[64,2048]{1,0:T(8,128)(2,1)S(1)} %get-tuple-element.8), channel_id=1, source_target_pairs={{0,14},{1,15},{2,0},{3,1},{4,2},{5,3},{6,4},{7,5},{8,6},{9,7},{10,... | collective-permute-start | bytes 786440 | tf_op jit(solution)/shard_map/ppermute | solution.py:109
  198.7 7.7 %collective-permute-start.16 = (bf16[64,2048]{1,0:T(8,128)(2,1)S(1)}, bf16[64,2048]{1,0:T(8,128)(2,1)S(1)}, u32[]{:S(2)}, u32[]{:S(2)}) collective-permute-start(bf16[64,2048]{1,0:T(8,128)(2,1)S(1)} %get-tuple-element.6), channel_id=1, source_target_pairs={{0,14},{1,15},{2,0},{3,1},{4,2},{5,3},{6,4},{7,5},{8,6},{9,7},{10,... | collective-permute-start | bytes 786440 | tf_op jit(solution)/shard_map/ppermute | solution.py:109
  198.8 7.6 %collective-permute-start.12 = (bf16[64,2048]{1,0:T(8,128)(2,1)S(1)}, bf16[64,2048]{1,0:T(8,128)(2,1)S(1)}, u32[]{:S(2)}, u32[]{:S(2)}) collective-permute-start(bf16[64,2048]{1,0:T(8,128)(2,1)S(1)} %get-tuple-element.5), channel_id=1, source_target_pairs={{0,2},{1,3},{2,4},{3,5},{4,6},{5,7},{6,8},{7,9},{8,10},{9,11},{10,... | collective-permute-start | bytes 786440 | tf_op jit(solution)/shard_map/ppermute | solution.py:109
  (1 other events, 1.1 us)

commit v2 on v1

v2 whole, which is shorter than its diff:
```python
import functools

import jax
import jax.numpy as jnp
from jax import lax
from jax.experimental import pallas as pl
from jax.experimental.pallas import tpu as pltpu
from jax.sharding import PartitionSpec as P

F32 = jnp.float32
BF16 = jnp.bfloat16
EXTRA = 128
VMEM = pl.BlockSpec(memory_space=pltpu.VMEM)
SMEM = pl.BlockSpec(memory_space=pltpu.SMEM)
PARAMS = pltpu.CompilerParams(vmem_limit_bytes=20 << 20)


def on_chip(x):
    return pltpu.with_memory_space_constraint(x, pltpu.VMEM)


def after(x, *others):
    return lax.optimization_barrier((x,) + others)[0]


def kernel_call(body, name, outs, arrays, scalars=(), keep=False):
    return pl.pallas_call(
        body,
        out_shape=[pltpu.VMEM(*out) if keep else jax.ShapeDtypeStruct(*out) for out in outs],
        in_specs=[SMEM] * len(scalars) + [VMEM] * len(arrays),
        out_specs=[VMEM] * len(outs),
        compiler_params=PARAMS,
        name=name,
    )(*scalars, *arrays)


def slot_of(index, slots):
    group = jnp.zeros_like(index)
    for d in range(1, 16):
        group = group + (index >= d * slots).astype(jnp.int32)
    return group, index - group * slots


def dispatch_kernel(slots, planes, z_ref, *refs):
    refs, out_ref, extra_ref = refs[:-2], refs[-2], refs[-1]
    width = out_ref.shape[1]
    groups = out_ref.shape[0] // slots
    extra = jnp.concatenate([x[:, width:] for x in refs], axis=0)
    extra_ref[...] = extra
    extra = extra.astype(F32).T
    tokens = extra.shape[1]
    dest = planes * lax.broadcasted_iota(jnp.int32, (groups, 1), 0) + z_ref[0]
    dest = dest.astype(F32)
    match = jnp.zeros((groups, tokens), F32)
    for k in range(8):
        match = match + (extra[k : k + 1, :] == dest).astype(F32)
    upper = lax.broadcasted_iota(jnp.int32, (tokens, tokens), 0) <= lax.broadcasted_iota(
        jnp.int32, (tokens, tokens), 1
    )
    upper = upper.astype(F32).astype(BF16)
    order = jnp.dot(match.astype(BF16), upper, preferred_element_type=F32) * match
    row = lax.broadcasted_iota(jnp.int32, (groups * slots, 1), 0)
    group, place = slot_of(row, slots)
    spread = (group == lax.broadcasted_iota(jnp.int32, (1, groups), 1)).astype(F32).astype(BF16)
    wanted = jnp.dot(spread, order.astype(BF16), preferred_element_type=F32)
    pick = (wanted == (place + 1).astype(F32)).astype(F32).astype(BF16)
    rows = jnp.concatenate([x[:, :width] for x in refs], axis=0)
    out_ref[...] = jnp.dot(pick, rows, preferred_element_type=F32).astype(BF16)


def expert_kernel(x_ref, g0, g1, u0, u1, d0, d1, out_ref):
    x = x_ref[...]
    total = None
    for g_ref, u_ref, d_ref in ((g0, u0, d0), (g1, u1, d1)):
        gate = jnp.dot(x, g_ref[...], preferred_element_type=F32)
        up = jnp.dot(x, u_ref[...], preferred_element_type=F32)
        hidden = (gate / (1.0 + jnp.exp(-gate)) * up).astype(BF16)
        part = jnp.dot(hidden, d_ref[...], preferred_element_type=F32)
        total = part if total is None else total + part
    out_ref[...] = total.astype(BF16)


def weights_kernel(slots, planes, z_ref, extra_ref, high_ref, low_ref):
    tokens, columns = high_ref.shape
    groups = columns // slots
    extra = extra_ref[...].astype(F32)
    gates = extra[:, 8:16] * 256.0 + extra[:, 16:24]
    mix = gates / jnp.sum(gates, axis=1, keepdims=True)
    dest = planes * lax.broadcasted_iota(jnp.int32, (1, EXTRA), 1) + z_ref[0]
    dest = dest.astype(F32)
    match = jnp.zeros((tokens, EXTRA), F32)
    weight = jnp.zeros((tokens, EXTRA), F32)
    for k in range(8):
        same = extra[:, k : k + 1] == dest
        match = match + same.astype(F32)
        weight = weight + jnp.where(same, mix[:, k : k + 1], 0.0)
    lower = lax.broadcasted_iota(jnp.int32, (tokens, tokens), 1) <= lax.broadcasted_iota(
        jnp.int32, (tokens, tokens), 0
    )
    lower = lower.astype(F32).astype(BF16)
    order = jnp.dot(lower, match.astype(BF16), preferred_element_type=F32) * match
    column = lax.broadcasted_iota(jnp.int32, (1, groups * slots), 1)
    group, place = slot_of(column, slots)
    spread = (group == lax.broadcasted_iota(jnp.int32, (EXTRA, 1), 0)).astype(F32).astype(BF16)
    wanted = jnp.dot(order.astype(BF16), spread, preferred_element_type=F32)
    here = wanted == (place + 1).astype(F32)
    high = weight.astype(BF16)
    low = (weight - high.astype(F32)).astype(BF16)
    for piece, ref in ((high, high_ref), (low, low_ref)):
        wide = jnp.dot(piece, spread, preferred_element_type=F32)
        ref[...] = jnp.where(here, wide, 0.0).astype(BF16)


def combine_kernel(home_ref, high_ref, low_ref, *outs):
    home = home_ref[...]
    total = jnp.dot(high_ref[...], home, preferred_element_type=F32)
    total = total + jnp.dot(low_ref[...], home, preferred_element_type=F32)
    start = 0
    for out in outs:
        rows = out.shape[0]
        out[...] = total[start : start + rows, :].astype(out.dtype)
        start += rows


def per_device(tokens, expert_ids, gate_fixed, w_gate, w_up, w_down):
    col_count = lax.axis_size("expert")
    dp_count = lax.axis_size("dp")
    planes = col_count // 2
    half = planes // 2
    all_rows, width = tokens.shape
    rows = all_rows // 2
    slots = 3 * planes * rows // 32
    plane = (lax.axis_index("expert") // 2).astype(jnp.int32).reshape(1)

    def along_z(x, by):
        return lax.ppermute(
            x, "expert", [(i, (i + 2 * by) % col_count) for i in range(col_count)]
        )

    def partner(x):
        return lax.ppermute(x, "expert", [(i, i ^ 1) for i in range(col_count)])

    packed = jnp.concatenate(
        [
            expert_ids,
            gate_fixed // 256,
            gate_fixed % 256,
            jnp.zeros((all_rows, EXTRA - 24), jnp.int32),
        ],
        axis=1,
    ).astype(BF16)
    mine = jnp.concatenate([tokens, packed], axis=1)

    def gather(own):
        up = down = own
        shards = [own]
        for step in range(half):
            up = along_z(up, 1)
            shards.append(up)
            if step < half - 1:
                down = along_z(down, -1)
                shards.append(down)
        return shards

    def exchange(x):
        return lax.all_to_all(x, "dp", split_axis=0, concat_axis=0, tiled=True)

    def dispatch(shards):
        return kernel_call(
            functools.partial(dispatch_kernel, slots, planes),
            "dispatch",
            [((dp_count * slots, width), BF16), ((planes * rows, EXTRA), BF16)],
            [on_chip(x) for x in shards],
            [plane],
        )

    def mixing(extra):
        shape = (planes * rows, dp_count * slots)
        return kernel_call(
            functools.partial(weights_kernel, slots, planes),
            "mixing",
            [(shape, BF16), (shape, BF16)],
            [extra],
            [plane],
        )

    def scatter(part):
        from_low = [part[2 * i - 1] for i in range(1, half + 1)]
        from_high = [part[2 * i] for i in range(1, half)]
        down = from_low[half - 1]
        up = from_high[half - 2]
        marks = []
        for step in range(half):
            down = along_z(down, -1)
            if step < half - 1:
                down = (down.astype(F32) + from_low[half - 2 - step]).astype(BF16)
                up = along_z(up, 1)
                if step < half - 2:
                    up = (up.astype(F32) + from_high[half - 3 - step]).astype(BF16)
            marks.append(down)
        return part[0] + up.astype(F32) + down.astype(F32), marks

    panels = []
    for w in (w_gate[0], w_up[0], w_down[0]):
        panels += [w, partner(w)]

    def expert(x):
        return kernel_call(expert_kernel, "expert", [(x.shape, BF16)], [x] + panels)[0]

    def combine(home, mix, keep):
        kinds = [F32] * (planes - 2) + [BF16] * 2
        outs = [((rows, width), kind) for kind in kinds]
        return kernel_call(combine_kernel, "combine", outs, [home] + list(mix), keep=keep)

    first = gather(mine[:rows])
    out_0, extra_0 = dispatch(first)
    there_0 = exchange(out_0)
    second = gather(after(mine[rows:], first[-2]))
    out_1, extra_1 = dispatch(second)
    there_0 = after(there_0, out_1)
    there_1 = exchange(out_1)
    done_0 = expert(there_0)
    done_0 = after(done_0, there_1)
    home_0 = exchange(done_0)
    mix_0, mix_1 = mixing(extra_0), mixing(extra_1)
    done_1 = after(expert(there_1), *mix_0, *mix_1)
    home_1 = exchange(done_1)
    mixed_0, marks = scatter(combine(home_0, mix_0, False))
    home_1 = after(home_1, marks[half - 2])
    mixed_1, _ = scatter(combine(home_1, mix_1, True))
    return jnp.concatenate([mixed_0, mixed_1], axis=0)


def solution(mesh):
    rows = P(("dp", "expert"), None)
    panels = P(("dp", "expert"), None, None)
    return jax.shard_map(
        per_device,
        mesh=mesh,
        in_specs=(rows, rows, rows, panels, panels, panels),
        out_specs=rows,
        check_vma=False,
    )
```

time: 211 us -> 199 us (0.943); the launches traced: 207 us -> 199 us
  waiting for transfers between devices: 126 us -> 82.4 us
  starting transfers between devices: 34.9 us -> 73.7 us
  Pallas kernels: 32 us -> 23.6 us
  local copies, waits for them, and re-layouts: 9.66 us -> 14.9 us
    all_to_all x2 -> x4, waiting for transfers between devices: 73.1 us -> 40.1 us  [exchange(): return lax.all_to_all(x, 'dp', split_axis=0, concat_axis=0, tiled=True)]
    ppermute x14 -> x28, starting transfers between devices: 23.3 us -> 50.8 us  [along_z(): lax.ppermute(x, 'expert', [(i, (i + 2 * by) % col_count) for i in range(c...]
    all_to_all x2 -> x4, starting transfers between devices: 11 us -> 22.3 us  [exchange(): return lax.all_to_all(x, 'dp', split_axis=0, concat_axis=0, tiled=True)]
    pallas_call x3 -> x8, Pallas kernels: 32 us -> 23.6 us  [kernel_call(): pl.pallas_call(body, out_shape=[pltpu.VMEM(*out) if keep else jax.ShapeDt...]
    ppermute x3, waiting for transfers between devices: 7.51 us -> 0.01 us  [partner(): return lax.ppermute(x, 'expert', [(i, i ^ 1) for i in range(col_count)])]
    unnamed x20 -> x53, local copies, waits for them, and re-layouts: 6.87 us -> 13.7 us
    ppermute x14 -> x28, waiting for transfers between devices: 45.3 us -> 42.3 us  [along_z(): lax.ppermute(x, 'expert', [(i, (i + 2 * by) % col_count) for i in range(c...]
    another operation x3 -> x2, other arithmetic: 3.39 us -> 0.73 us
  transfers between devices with their start and end apart: 19 -> 35, of which waited for: 13 -> 18; matrix products, arithmetic and copies ran while one was open for 1% -> 1% of each run, Pallas kernels for 0% -> 10%
where the time goes in v2:
time: 199 us
  waiting for transfers between devices  82.4 us (41%)
  starting transfers between devices  73.7 us (37%)
  Pallas kernels  23.6 us (12%)
  local copies, waits for them, and re-layouts  14.9 us (7%)
  other arithmetic  3.47 us (2%)
    ppermute x28, starting transfers between devices, along_z(): lax.ppermute(x, 'expert', [(i, (i + 2 * by) % col_count) for i in range(c...  50.8 us
    ppermute x28, waiting for transfers between devices, along_z(): lax.ppermute(x, 'expert', [(i, (i + 2 * by) % col_count) for i in range(c...  42.3 us
    all_to_all x4, waiting for transfers between devices, exchange(): return lax.all_to_all(x, 'dp', split_axis=0, concat_axis=0, tiled=True)  40.1 us
    pallas_call x8, Pallas kernels, kernel_call(): pl.pallas_call(body, out_shape=[pltpu.VMEM(*out) if keep else jax.ShapeDt...  23.6 us
    all_to_all x4, starting transfers between devices, exchange(): return lax.all_to_all(x, 'dp', split_axis=0, concat_axis=0, tiled=True)  22.3 us
    unnamed x53, local copies, waits for them, and re-layouts  13.7 us
  transfers between devices with their start and end apart: 35, of which 18 were waited for; matrix products, arithmetic and copies ran while one was open for 1% of the time, Pallas kernels for 10%

profile of v2, /device:TPU:96, one launch (start us, length us, event | category | flops | bytes accessed | tf_op | source)
XLA Modules:
  0.0 198.5 jit_solution(1937042757849446640)
XLA Ops:
  8.8 3.7 %collective-permute-start.2 = (bf16[32,2176]{1,0:T(8,128)(2,1)S(1)}, bf16[32,2176]{1,0:T(8,128)(2,1)S(1)}, u32[]{:S(2)}, u32[]{:S(2)}) collective-permute-start(bf16[32,2176]{1,0:T(8,128)(2,1)S(1)} %collective-permute-done.refs_1_), channel_id=1, source_target_pairs={{0,2},{1,3},{2,4},{3,5},{4,6},{5,7},{6,8},{7,9},{8,10},{9,11},{10,... | collective-permute-start | bytes 417800 | tf_op jit(solution)/shard_map/ppermute | solution.py:136
  15.1 3.7 %collective-permute-start.4 = (bf16[32,2176]{1,0:T(8,128)(2,1)S(1)}, bf16[32,2176]{1,0:T(8,128)(2,1)S(1)}, u32[]{:S(2)}, u32[]{:S(2)}) collective-permute-start(bf16[32,2176]{1,0:T(8,128)(2,1)S(1)} %collective-permute-done.2.refs_3_), channel_id=1, source_target_pairs={{0,2},{1,3},{2,4},{3,5},{4,6},{5,7},{6,8},{7,9},{8,10},{9,11},{10,... | collective-permute-start | bytes 417800 | tf_op jit(solution)/shard_map/ppermute | solution.py:136
  21.4 3.7 %collective-permute-start.6 = (bf16[32,2176]{1,0:T(8,128)(2,1)S(1)}, bf16[32,2176]{1,0:T(8,128)(2,1)S(1)}, u32[]{:S(2)}, u32[]{:S(2)}) collective-permute-start(bf16[32,2176]{1,0:T(8,128)(2,1)S(1)} %collective-permute-done.4.refs_5_), channel_id=1, source_target_pairs={{0,2},{1,3},{2,4},{3,5},{4,6},{5,7},{6,8},{7,9},{8,10},{9,11},{10,... | collective-permute-start | bytes 417800 | tf_op jit(solution)/shard_map/ppermute | solution.py:136
  29.7 7.3 %all-to-all-start = ((bf16[16,24,2048]{2,1,0:T(8,128)(2,1)}), bf16[16,24,2048]{2,1,0:T(8,128)(2,1)}, u32[]{:S(2)}, u32[]{:S(2)}) async-start(bf16[16,24,2048]{2,1,0:T(8,128)(2,1)} %bitcast.24), calls=%async_computation | async-start | bytes 3145728 | tf_op jit(solution)/shard_map/all_to_all | solution.py:166
  37.1 3.8 %collective-permute-start.7 = (bf16[32,2176]{1,0:T(8,128)(2,1)S(1)}, bf16[32,2176]{1,0:T(8,128)(2,1)S(1)}, u32[]{:S(2)}, u32[]{:S(2)}) collective-permute-start(bf16[32,2176]{1,0:T(8,128)(2,1)S(1)} %get-tuple-element.35.refs_0_), channel_id=1, source_target_pairs={{0,2},{1,3},{2,4},{3,5},{4,6},{5,7},{6,8},{7,9},{8,10},{9,11},{10,... | collective-permute-start | bytes 417800 | tf_op jit(solution)/shard_map/ppermute | solution.py:136
  40.9 3.4 %collective-permute-done.7.refs_1_ = bf16[32,2176]{1,0:T(8,128)(2,1)S(1)} collective-permute-done((bf16[32,2176]{1,0:T(8,128)(2,1)S(1)}, bf16[32,2176]{1,0:T(8,128)(2,1)S(1)}, u32[]{:S(2)}, u32[]{:S(2)}) %collective-permute-start.7) | collective-permute-done | bytes 139296 | tf_op jit(solution)/shard_map/ppermute | solution.py:136
  44.3 3.7 %collective-permute-start.9 = (bf16[32,2176]{1,0:T(8,128)(2,1)S(1)}, bf16[32,2176]{1,0:T(8,128)(2,1)S(1)}, u32[]{:S(2)}, u32[]{:S(2)}) collective-permute-start(bf16[32,2176]{1,0:T(8,128)(2,1)S(1)} %collective-permute-done.7.refs_1_), channel_id=1, source_target_pairs={{0,2},{1,3},{2,4},{3,5},{4,6},{5,7},{6,8},{7,9},{8,10},{9,11},{10,... | collective-permute-start | bytes 417800 | tf_op jit(solution)/shard_map/ppermute | solution.py:136
  50.7 3.7 %collective-permute-start.11 = (bf16[32,2176]{1,0:T(8,128)(2,1)S(1)}, bf16[32,2176]{1,0:T(8,128)(2,1)S(1)}, u32[]{:S(2)}, u32[]{:S(2)}) collective-permute-start(bf16[32,2176]{1,0:T(8,128)(2,1)S(1)} %collective-permute-done.9.refs_3_), channel_id=1, source_target_pairs={{0,2},{1,3},{2,4},{3,5},{4,6},{5,7},{6,8},{7,9},{8,10},{9,11},{10,... | collective-permute-start | bytes 417800 | tf_op jit(solution)/shard_map/ppermute | solution.py:136
  57.0 3.7 %collective-permute-start.13 = (bf16[32,2176]{1,0:T(8,128)(2,1)S(1)}, bf16[32,2176]{1,0:T(8,128)(2,1)S(1)}, u32[]{:S(2)}, u32[]{:S(2)}) collective-permute-start(bf16[32,2176]{1,0:T(8,128)(2,1)S(1)} %collective-permute-done.11.refs_5_), channel_id=1, source_target_pairs={{0,2},{1,3},{2,4},{3,5},{4,6},{5,7},{6,8},{7,9},{8,10},{9,11},{10,... | collective-permute-start | bytes 417800 | tf_op jit(solution)/shard_map/ppermute | solution.py:136
  65.4 6.7 %all-to-all-start.1 = ((bf16[16,24,2048]{2,1,0:T(8,128)(2,1)}), bf16[16,24,2048]{2,1,0:T(8,128)(2,1)}, u32[]{:S(2)}, u32[]{:S(2)}) async-start(bf16[16,24,2048]{2,1,0:T(8,128)(2,1)} %bitcast.25), calls=%async_computation.1 | async-start | bytes 3145728 | tf_op jit(solution)/shard_map/all_to_all | solution.py:166
  73.5 7.9 %expert.2 = bf16[384,2048]{1,0:T(8,128)(2,1)S(1)} custom-call(bf16[384,2048]{1,0:T(8,128)(2,1)} %bitcast.2.x_ref, bf16[2048,384]{1,0:T(8,128)(2,1)S(1)} %bitcast.13, bf16[2048,384]{1,0:T(8,128)(2,1)} %collective-permute-done.14.g1, bf16[2048,384]{1,0:T(8,128)(2,1)S(1)} %bitcast.16, bf16[2048,384]{1,0:T(8,128)(2,1)} %collective-permute-done.15.u1, ...), custom_call_target="tpu_custom_call" | custom-call | tf_op jit(solution)/shard_map/expert/pallas_call | solution.py:27
  82.6 11.6 %all-to-all-done.1 = bf16[16,24,2048]{2,1,0:T(8,128)(2,1)} async-done(((bf16[16,24,2048]{2,1,0:T(8,128)(2,1)}), bf16[16,24,2048]{2,1,0:T(8,128)(2,1)}, u32[]{:S(2)}, u32[]{:S(2)}) %all-to-all-start.1) | async-done | bytes 1572896 | tf_op jit(solution)/shard_map/all_to_all | solution.py:166
  94.2 4.4 %all-to-all-start.2 = ((bf16[16,24,2048]{2,1,0:T(8,128)(2,1)}), bf16[16,24,2048]{2,1,0:T(8,128)(2,1)}, u32[]{:S(2)}, u32[]{:S(2)}) async-start(bf16[16,24,2048]{2,1,0:T(8,128)(2,1)} %bitcast.22), calls=%async_computation.2 | async-start | bytes 3145728 | tf_op jit(solution)/shard_map/all_to_all | solution.py:166
  101.1 19.2 %all-to-all-done.2 = bf16[16,24,2048]{2,1,0:T(8,128)(2,1)} async-done(((bf16[16,24,2048]{2,1,0:T(8,128)(2,1)}), bf16[16,24,2048]{2,1,0:T(8,128)(2,1)}, u32[]{:S(2)}, u32[]{:S(2)}) %all-to-all-start.2) | async-done | bytes 1572896 | tf_op jit(solution)/shard_map/all_to_all | solution.py:166
  127.0 7.6 %collective-permute-done.20 = bf16[32,2048]{1,0:T(8,128)(2,1)S(1)} collective-permute-done((bf16[32,2048]{1,0:T(8,128)(2,1)S(1)}, bf16[32,2048]{1,0:T(8,128)(2,1)S(1)}, u32[]{:S(2)}, u32[]{:S(2)}) %collective-permute-start.20) | collective-permute-done | bytes 131104 | tf_op jit(solution)/shard_map/ppermute | solution.py:136
  137.7 7.9 %expert.3 = bf16[384,2048]{1,0:T(8,128)(2,1)S(1)} custom-call(bf16[384,2048]{1,0:T(8,128)(2,1)} %bitcast.7.x_ref, bf16[2048,384]{1,0:T(8,128)(2,1)S(1)} %bitcast.14, bf16[2048,384]{1,0:T(8,128)(2,1)} %collective-permute-done.14.g1, bf16[2048,384]{1,0:T(8,128)(2,1)S(1)} %bitcast.17, bf16[2048,384]{1,0:T(8,128)(2,1)} %collective-permute-done.15.u1, ...), custom_call_target="tpu_custom_call" | custom-call | tf_op jit(solution)/shard_map/expert/pallas_call | solution.py:27
  146.9 3.9 %all-to-all-start.3 = ((bf16[16,24,2048]{2,1,0:T(8,128)(2,1)}), bf16[16,24,2048]{2,1,0:T(8,128)(2,1)S(1)}, u32[]{:S(2)}, u32[]{:S(2)}) async-start(bf16[16,24,2048]{2,1,0:T(8,128)(2,1)} %bitcast.21), calls=%async_computation.3 | async-start | bytes 3145728 | tf_op jit(solution)/shard_map/all_to_all | solution.py:166
  150.8 3.3 %collective-permute-start.17 = (bf16[32,2048]{1,0:T(8,128)(2,1)S(1)}, bf16[32,2048]{1,0:T(8,128)(2,1)S(1)}, u32[]{:S(2)}, u32[]{:S(2)}) collective-permute-start(bf16[32,2048]{1,0:T(8,128)(2,1)S(1)} %copy-done.25), channel_id=1, source_target_pairs={{0,2},{1,3},{2,4},{3,5},{4,6},{5,7},{6,8},{7,9},{8,10},{9,11},{10,... | collective-permute-start | bytes 393224 | tf_op jit(solution)/shard_map/ppermute | solution.py:136
  156.8 3.8 %collective-permute-start.18 = (bf16[32,2048]{1,0:T(8,128)(2,1)S(1)}, bf16[32,2048]{1,0:T(8,128)(2,1)S(1)}, u32[]{:S(2)}, u32[]{:S(2)}) collective-permute-start(bf16[32,2048]{1,0:T(8,128)(2,1)S(1)} %add_convert_fusion.9), channel_id=1, source_target_pairs={{0,2},{1,3},{2,4},{3,5},{4,6},{5,7},{6,8},{7,9},{8,10},{9,11},{10,... | collective-permute-start | bytes 393224 | tf_op jit(solution)/shard_map/ppermute | solution.py:136
  161.3 9.3 %all-to-all-done.3 = bf16[16,24,2048]{2,1,0:T(8,128)(2,1)S(1)} async-done(((bf16[16,24,2048]{2,1,0:T(8,128)(2,1)}), bf16[16,24,2048]{2,1,0:T(8,128)(2,1)S(1)}, u32[]{:S(2)}, u32[]{:S(2)}) %all-to-all-start.3) | async-done | bytes 1572896 | tf_op jit(solution)/shard_map/all_to_all | solution.py:166
  172.0 3.3 %collective-permute-start.19 = (bf16[32,2048]{1,0:T(8,128)(2,1)S(1)}, bf16[32,2048]{1,0:T(8,128)(2,1)S(1)}, u32[]{:S(2)}, u32[]{:S(2)}) collective-permute-start(bf16[32,2048]{1,0:T(8,128)(2,1)S(1)} %add_convert_fusion.8), channel_id=1, source_target_pairs={{0,2},{1,3},{2,4},{3,5},{4,6},{5,7},{6,8},{7,9},{8,10},{9,11},{10,... | collective-permute-start | bytes 393224 | tf_op jit(solution)/shard_map/ppermute | solution.py:136
  181.1 4.0 %collective-permute-start.25 = (bf16[32,2048]{1,0:T(8,128)(2,1)S(1)}, bf16[32,2048]{1,0:T(8,128)(2,1)S(1)}, u32[]{:S(2)}, u32[]{:S(2)}) collective-permute-start(bf16[32,2048]{1,0:T(8,128)(2,1)S(1)} %add_convert_fusion.4), channel_id=1, source_target_pairs={{0,2},{1,3},{2,4},{3,5},{4,6},{5,7},{6,8},{7,9},{8,10},{9,11},{10,... | collective-permute-start | bytes 393224 | tf_op jit(solution)/shard_map/ppermute | solution.py:136
  187.6 3.7 %collective-permute-start.26 = (bf16[32,2048]{1,0:T(8,128)(2,1)S(1)}, bf16[32,2048]{1,0:T(8,128)(2,1)S(1)}, u32[]{:S(2)}, u32[]{:S(2)}) collective-permute-start(bf16[32,2048]{1,0:T(8,128)(2,1)S(1)} %add_convert_fusion.3), channel_id=1, source_target_pairs={{0,2},{1,3},{2,4},{3,5},{4,6},{5,7},{6,8},{7,9},{8,10},{9,11},{10,... | collective-permute-start | bytes 393224 | tf_op jit(solution)/shard_map/ppermute | solution.py:136
  193.9 3.8 %collective-permute-done.30 = bf16[32,2048]{1,0:T(8,128)(2,1)S(1)} collective-permute-done((bf16[32,2048]{1,0:T(8,128)(2,1)S(1)}, bf16[32,2048]{1,0:T(8,128)(2,1)S(1)}, u32[]{:S(2)}, u32[]{:S(2)}) %collective-permute-start.30) | collective-permute-done | bytes 131104 | tf_op jit(solution)/shard_map/ppermute | solution.py:136
  (126 shorter events, 61.2 us)
Async XLA Ops:
  5.9 6.6 %collective-permute-start.1 = (bf16[32,2176]{1,0:T(8,128)(2,1)S(1)}, bf16[32,2176]{1,0:T(8,128)(2,1)S(1)}, u32[]{:S(2)}, u32[]{:S(2)}) collective-permute-start(bf16[32,2176]{1,0:T(8,128)(2,1)S(1)} %get-tuple-element.63.refs_0_), channel_id=1, source_target_pairs={{0,14},{1,15},{2,0},{3,1},{4,2},{5,3},{6,4},{7,5},{8,6},{9,7},{10,... | collective-permute-start | bytes 417800 | tf_op jit(solution)/shard_map/ppermute | solution.py:136
  8.8 6.3 %collective-permute-start.2 = (bf16[32,2176]{1,0:T(8,128)(2,1)S(1)}, bf16[32,2176]{1,0:T(8,128)(2,1)S(1)}, u32[]{:S(2)}, u32[]{:S(2)}) collective-permute-start(bf16[32,2176]{1,0:T(8,128)(2,1)S(1)} %collective-permute-done.refs_1_), channel_id=1, source_target_pairs={{0,2},{1,3},{2,4},{3,5},{4,6},{5,7},{6,8},{7,9},{8,10},{9,11},{10,... | collective-permute-start | bytes 417800 | tf_op jit(solution)/shard_map/ppermute | solution.py:136
  12.5 6.3 %collective-permute-start.3 = (bf16[32,2176]{1,0:T(8,128)(2,1)S(1)}, bf16[32,2176]{1,0:T(8,128)(2,1)S(1)}, u32[]{:S(2)}, u32[]{:S(2)}) collective-permute-start(bf16[32,2176]{1,0:T(8,128)(2,1)S(1)} %collective-permute-done.1.refs_2_), channel_id=1, source_target_pairs={{0,14},{1,15},{2,0},{3,1},{4,2},{5,3},{6,4},{7,5},{8,6},{9,7},{10,... | collective-permute-start | bytes 417800 | tf_op jit(solution)/shard_map/ppermute | solution.py:136
  29.7 35.6 %all-to-all-start = ((bf16[16,24,2048]{2,1,0:T(8,128)(2,1)}), bf16[16,24,2048]{2,1,0:T(8,128)(2,1)}, u32[]{:S(2)}, u32[]{:S(2)}) async-start(bf16[16,24,2048]{2,1,0:T(8,128)(2,1)} %bitcast.24), calls=%async_computation | async-start | bytes 3145728 | tf_op jit(solution)/shard_map/all_to_all | solution.py:166
  37.1 7.2 %collective-permute-start.7 = (bf16[32,2176]{1,0:T(8,128)(2,1)S(1)}, bf16[32,2176]{1,0:T(8,128)(2,1)S(1)}, u32[]{:S(2)}, u32[]{:S(2)}) collective-permute-start(bf16[32,2176]{1,0:T(8,128)(2,1)S(1)} %get-tuple-element.35.refs_0_), channel_id=1, source_target_pairs={{0,2},{1,3},{2,4},{3,5},{4,6},{5,7},{6,8},{7,9},{8,10},{9,11},{10,... | collective-permute-start | bytes 417800 | tf_op jit(solution)/shard_map/ppermute | solution.py:136
  40.8 7.1 %collective-permute-start.8 = (bf16[32,2176]{1,0:T(8,128)(2,1)S(1)}, bf16[32,2176]{1,0:T(8,128)(2,1)S(1)}, u32[]{:S(2)}, u32[]{:S(2)}) collective-permute-start(bf16[32,2176]{1,0:T(8,128)(2,1)S(1)} %get-tuple-element.35.refs_0_), channel_id=1, source_target_pairs={{0,14},{1,15},{2,0},{3,1},{4,2},{5,3},{6,4},{7,5},{8,6},{9,7},{10,... | collective-permute-start | bytes 417800 | tf_op jit(solution)/shard_map/ppermute | solution.py:136
  44.3 6.4 %collective-permute-start.9 = (bf16[32,2176]{1,0:T(8,128)(2,1)S(1)}, bf16[32,2176]{1,0:T(8,128)(2,1)S(1)}, u32[]{:S(2)}, u32[]{:S(2)}) collective-permute-start(bf16[32,2176]{1,0:T(8,128)(2,1)S(1)} %collective-permute-done.7.refs_1_), channel_id=1, source_target_pairs={{0,2},{1,3},{2,4},{3,5},{4,6},{5,7},{6,8},{7,9},{8,10},{9,11},{10,... | collective-permute-start | bytes 417800 | tf_op jit(solution)/shard_map/ppermute | solution.py:136
  48.0 6.4 %collective-permute-start.10 = (bf16[32,2176]{1,0:T(8,128)(2,1)S(1)}, bf16[32,2176]{1,0:T(8,128)(2,1)S(1)}, u32[]{:S(2)}, u32[]{:S(2)}) collective-permute-start(bf16[32,2176]{1,0:T(8,128)(2,1)S(1)} %collective-permute-done.8.refs_2_), channel_id=1, source_target_pairs={{0,14},{1,15},{2,0},{3,1},{4,2},{5,3},{6,4},{7,5},{8,6},{9,7},{10,... | collective-permute-start | bytes 417800 | tf_op jit(solution)/shard_map/ppermute | solution.py:136
  50.7 6.3 %collective-permute-start.11 = (bf16[32,2176]{1,0:T(8,128)(2,1)S(1)}, bf16[32,2176]{1,0:T(8,128)(2,1)S(1)}, u32[]{:S(2)}, u32[]{:S(2)}) collective-permute-start(bf16[32,2176]{1,0:T(8,128)(2,1)S(1)} %collective-permute-done.9.refs_3_), channel_id=1, source_target_pairs={{0,2},{1,3},{2,4},{3,5},{4,6},{5,7},{6,8},{7,9},{8,10},{9,11},{10,... | collective-permute-start | bytes 417800 | tf_op jit(solution)/shard_map/ppermute | solution.py:136
  54.4 6.9 %collective-permute-start.12 = (bf16[32,2176]{1,0:T(8,128)(2,1)S(1)}, bf16[32,2176]{1,0:T(8,128)(2,1)S(1)}, u32[]{:S(2)}, u32[]{:S(2)}) collective-permute-start(bf16[32,2176]{1,0:T(8,128)(2,1)S(1)} %collective-permute-done.10.refs_4_), channel_id=1, source_target_pairs={{0,14},{1,15},{2,0},{3,1},{4,2},{5,3},{6,4},{7,5},{8,6},{9,7},{10,... | collective-permute-start | bytes 417800 | tf_op jit(solution)/shard_map/ppermute | solution.py:136
  60.7 11.4 %collective-permute-start.14 = (bf16[2048,384]{1,0:T(8,128)(2,1)S(1)}, bf16[2048,384]{1,0:T(8,128)(2,1)}, u32[]{:S(2)}, u32[]{:S(2)}) collective-permute-start(bf16[2048,384]{1,0:T(8,128)(2,1)S(1)} %bitcast.12), channel_id=1, source_target_pairs={{0,1},{1,0},{2,3},{3,2},{4,5},{5,4},{6,7},{7,6},{8,9},{9,8},{10,11... | collective-permute-start | bytes 4718600 | tf_op jit(solution)/shard_map/ppermute | solution.py:141
  60.7 11.4 %collective-permute-start.15 = (bf16[2048,384]{1,0:T(8,128)(2,1)S(1)}, bf16[2048,384]{1,0:T(8,128)(2,1)}, u32[]{:S(2)}, u32[]{:S(2)}) collective-permute-start(bf16[2048,384]{1,0:T(8,128)(2,1)S(1)} %bitcast.15), channel_id=1, source_target_pairs={{0,1},{1,0},{2,3},{3,2},{4,5},{5,4},{6,7},{7,6},{8,9},{9,8},{10,11... | collective-permute-start | bytes 4718600 | tf_op jit(solution)/shard_map/ppermute | solution.py:141
  61.2 10.9 %collective-permute-start.16 = (bf16[384,2048]{1,0:T(8,128)(2,1)}, bf16[384,2048]{1,0:T(8,128)(2,1)}, u32[]{:S(2)}, u32[]{:S(2)}) collective-permute-start(bf16[384,2048]{1,0:T(8,128)(2,1)} %bitcast.18), channel_id=1, source_target_pairs={{0,1},{1,0},{2,3},{3,2},{4,5},{5,4},{6,7},{7,6},{8,9},{9,8},{10,11... | collective-permute-start | bytes 4718600 | tf_op jit(solution)/shard_map/ppermute | solution.py:141
  65.4 28.9 %all-to-all-start.1 = ((bf16[16,24,2048]{2,1,0:T(8,128)(2,1)}), bf16[16,24,2048]{2,1,0:T(8,128)(2,1)}, u32[]{:S(2)}, u32[]{:S(2)}) async-start(bf16[16,24,2048]{2,1,0:T(8,128)(2,1)} %bitcast.25), calls=%async_computation.1 | async-start | bytes 3145728 | tf_op jit(solution)/shard_map/all_to_all | solution.py:166
  94.2 26.1 %all-to-all-start.2 = ((bf16[16,24,2048]{2,1,0:T(8,128)(2,1)}), bf16[16,24,2048]{2,1,0:T(8,128)(2,1)}, u32[]{:S(2)}, u32[]{:S(2)}) async-start(bf16[16,24,2048]{2,1,0:T(8,128)(2,1)} %bitcast.22), calls=%async_computation.2 | async-start | bytes 3145728 | tf_op jit(solution)/shard_map/all_to_all | solution.py:166
  127.0 7.6 %collective-permute-start.20 = (bf16[32,2048]{1,0:T(8,128)(2,1)S(1)}, bf16[32,2048]{1,0:T(8,128)(2,1)S(1)}, u32[]{:S(2)}, u32[]{:S(2)}) collective-permute-start(bf16[32,2048]{1,0:T(8,128)(2,1)S(1)} %get-tuple-element.46), channel_id=1, source_target_pairs={{0,14},{1,15},{2,0},{3,1},{4,2},{5,3},{6,4},{7,5},{8,6},{9,7},{10,... | collective-permute-start | bytes 393224 | tf_op jit(solution)/shard_map/ppermute | solution.py:136
  135.2 18.8 %collective-permute-start.21 = (bf16[32,2048]{1,0:T(8,128)(2,1)}, bf16[32,2048]{1,0:T(8,128)(2,1)}, u32[]{:S(2)}, u32[]{:S(2)}) collective-permute-start(bf16[32,2048]{1,0:T(8,128)(2,1)} %add_convert_fusion.7), channel_id=1, source_target_pairs={{0,14},{1,15},{2,0},{3,1},{4,2},{5,3},{6,4},{7,5},{8,6},{9,7},{10,... | collective-permute-start | bytes 393224 | tf_op jit(solution)/shard_map/ppermute | solution.py:136
  146.9 23.7 %all-to-all-start.3 = ((bf16[16,24,2048]{2,1,0:T(8,128)(2,1)}), bf16[16,24,2048]{2,1,0:T(8,128)(2,1)S(1)}, u32[]{:S(2)}, u32[]{:S(2)}) async-start(bf16[16,24,2048]{2,1,0:T(8,128)(2,1)} %bitcast.21), calls=%async_computation.3 | async-start | bytes 3145728 | tf_op jit(solution)/shard_map/all_to_all | solution.py:166
  156.8 15.2 %collective-permute-start.18 = (bf16[32,2048]{1,0:T(8,128)(2,1)S(1)}, bf16[32,2048]{1,0:T(8,128)(2,1)S(1)}, u32[]{:S(2)}, u32[]{:S(2)}) collective-permute-start(bf16[32,2048]{1,0:T(8,128)(2,1)S(1)} %add_convert_fusion.9), channel_id=1, source_target_pairs={{0,2},{1,3},{2,4},{3,5},{4,6},{5,7},{6,8},{7,9},{8,10},{9,11},{10,... | collective-permute-start | bytes 393224 | tf_op jit(solution)/shard_map/ppermute | solution.py:136
  171.9 6.7 %collective-permute-start.27 = (bf16[32,2048]{1,0:T(8,128)(2,1)S(1)}, bf16[32,2048]{1,0:T(8,128)(2,1)S(1)}, u32[]{:S(2)}, u32[]{:S(2)}) collective-permute-start(bf16[32,2048]{1,0:T(8,128)(2,1)S(1)} %get-tuple-element.59), channel_id=1, source_target_pairs={{0,14},{1,15},{2,0},{3,1},{4,2},{5,3},{6,4},{7,5},{8,6},{9,7},{10,... | collective-permute-start | bytes 393224 | tf_op jit(solution)/shard_map/ppermute | solution.py:136
  172.0 19.5 %collective-permute-start.19 = (bf16[32,2048]{1,0:T(8,128)(2,1)S(1)}, bf16[32,2048]{1,0:T(8,128)(2,1)S(1)}, u32[]{:S(2)}, u32[]{:S(2)}) collective-permute-start(bf16[32,2048]{1,0:T(8,128)(2,1)S(1)} %add_convert_fusion.8), channel_id=1, source_target_pairs={{0,2},{1,3},{2,4},{3,5},{4,6},{5,7},{6,8},{7,9},{8,10},{9,11},{10,... | collective-permute-start | bytes 393224 | tf_op jit(solution)/shard_map/ppermute | solution.py:136
  175.3 16.2 %collective-permute-start.23 = (bf16[32,2048]{1,0:T(8,128)(2,1)S(1)}, bf16[32,2048]{1,0:T(8,128)(2,1)S(1)}, u32[]{:S(2)}, u32[]{:S(2)}) collective-permute-start(bf16[32,2048]{1,0:T(8,128)(2,1)S(1)} %add_convert_fusion.5), channel_id=1, source_target_pairs={{0,14},{1,15},{2,0},{3,1},{4,2},{5,3},{6,4},{7,5},{8,6},{9,7},{10,... | collective-permute-start | bytes 393224 | tf_op jit(solution)/shard_map/ppermute | solution.py:136
  178.6 6.5 %collective-permute-start.28 = (bf16[32,2048]{1,0:T(8,128)(2,1)S(1)}, bf16[32,2048]{1,0:T(8,128)(2,1)S(1)}, u32[]{:S(2)}, u32[]{:S(2)}) collective-permute-start(bf16[32,2048]{1,0:T(8,128)(2,1)S(1)} %add_convert_fusion.2), channel_id=1, source_target_pairs={{0,14},{1,15},{2,0},{3,1},{4,2},{5,3},{6,4},{7,5},{8,6},{9,7},{10,... | collective-permute-start | bytes 393224 | tf_op jit(solution)/shard_map/ppermute | solution.py:136
  181.1 6.5 %collective-permute-start.25 = (bf16[32,2048]{1,0:T(8,128)(2,1)S(1)}, bf16[32,2048]{1,0:T(8,128)(2,1)S(1)}, u32[]{:S(2)}, u32[]{:S(2)}) collective-permute-start(bf16[32,2048]{1,0:T(8,128)(2,1)S(1)} %add_convert_fusion.4), channel_id=1, source_target_pairs={{0,2},{1,3},{2,4},{3,5},{4,6},{5,7},{6,8},{7,9},{8,10},{9,11},{10,... | collective-permute-start | bytes 393224 | tf_op jit(solution)/shard_map/ppermute | solution.py:136
  (37 other events, 269.0 us)

commit v3 on v2

--- a/solution.py
+++ b/solution.py
@@ -127,9 +127,8 @@
     dp_count = lax.axis_size("dp")
     planes = col_count // 2
     half = planes // 2
-    all_rows, width = tokens.shape
-    rows = all_rows // 2
-    slots = 3 * planes * rows // 32
+    rows, width = tokens.shape
+    slots = 3 * half * rows // 32
     plane = (lax.axis_index("expert") // 2).astype(jnp.int32).reshape(1)
 
     def along_z(x, by):
@@ -145,23 +144,12 @@
             expert_ids,
             gate_fixed // 256,
             gate_fixed % 256,
-            jnp.zeros((all_rows, EXTRA - 24), jnp.int32),
+            jnp.zeros((rows, EXTRA - 24), jnp.int32),
         ],
         axis=1,
     ).astype(BF16)
     mine = jnp.concatenate([tokens, packed], axis=1)
 
-    def gather(own):
-        up = down = own
-        shards = [own]
-        for step in range(half):
-            up = along_z(up, 1)
-            shards.append(up)
-            if step < half - 1:
-                down = along_z(down, -1)
-                shards.append(down)
-        return shards
-
     def exchange(x):
         return lax.all_to_all(x, "dp", split_axis=0, concat_axis=0, tiled=True)
 
@@ -169,13 +157,13 @@
         return kernel_call(
             functools.partial(dispatch_kernel, slots, planes),
             "dispatch",
-            [((dp_count * slots, width), BF16), ((planes * rows, EXTRA), BF16)],
+            [((dp_count * slots, width), BF16), ((half * rows, EXTRA), BF16)],
             [on_chip(x) for x in shards],
             [plane],
         )
 
     def mixing(extra):
-        shape = (planes * rows, dp_count * slots)
+        shape = (half * rows, dp_count * slots)
         return kernel_call(
             functools.partial(weights_kernel, slots, planes),
             "mixing",
@@ -184,22 +172,6 @@
             [plane],
         )
 
-    def scatter(part):
-        from_low = [part[2 * i - 1] for i in range(1, half + 1)]
-        from_high = [part[2 * i] for i in range(1, half)]
-        down = from_low[half - 1]
-        up = from_high[half - 2]
-        marks = []
-        for step in range(half):
-            down = along_z(down, -1)
-            if step < half - 1:
-                down = (down.astype(F32) + from_low[half - 2 - step]).astype(BF16)
-                up = along_z(up, 1)
-                if step < half - 2:
-                    up = (up.astype(F32) + from_high[half - 3 - step]).astype(BF16)
-            marks.append(down)
-        return part[0] + up.astype(F32) + down.astype(F32), marks
-
     panels = []
     for w in (w_gate[0], w_up[0], w_down[0]):
         panels += [w, partner(w)]
@@ -207,28 +179,36 @@
     def expert(x):
         return kernel_call(expert_kernel, "expert", [(x.shape, BF16)], [x] + panels)[0]
 
-    def combine(home, mix, keep):
-        kinds = [F32] * (planes - 2) + [BF16] * 2
+    def combine(home, mix, kinds, keep):
         outs = [((rows, width), kind) for kind in kinds]
         return kernel_call(combine_kernel, "combine", outs, [home] + list(mix), keep=keep)
 
-    first = gather(mine[:rows])
-    out_0, extra_0 = dispatch(first)
-    there_0 = exchange(out_0)
-    second = gather(after(mine[rows:], first[-2]))
-    out_1, extra_1 = dispatch(second)
-    there_0 = after(there_0, out_1)
-    there_1 = exchange(out_1)
-    done_0 = expert(there_0)
-    done_0 = after(done_0, there_1)
-    home_0 = exchange(done_0)
-    mix_0, mix_1 = mixing(extra_0), mixing(extra_1)
-    done_1 = after(expert(there_1), *mix_0, *mix_1)
-    home_1 = exchange(done_1)
-    mixed_0, marks = scatter(combine(home_0, mix_0, False))
-    home_1 = after(home_1, marks[half - 2])
-    mixed_1, _ = scatter(combine(home_1, mix_1, True))
-    return jnp.concatenate([mixed_0, mixed_1], axis=0)
+    def plus(x, part):
+        return (x.astype(F32) + part).astype(BF16)
+
+    low_1, high_1 = along_z(mine, 1), along_z(mine, -1)
+    low_2, high_2 = along_z(low_1, 1), along_z(high_1, -1)
+    low_3, high_3 = along_z(low_2, 1), along_z(high_2, -1)
+    low_4 = along_z(low_3, 1)
+
+    near_rows, near_extra = dispatch([mine, low_1, high_1, low_2])
+    near = exchange(after(near_rows, high_2))
+    far_rows, far_extra = dispatch([high_2, low_3, high_3, low_4])
+    near = after(near, far_rows)
+    far = exchange(far_rows)
+    near_out = after(expert(near), far)
+    near_mix, far_mix = mixing(near_extra), mixing(far_extra)
+    far_out = after(expert(far), near_out, *near_mix, *far_mix)
+    far_home = exchange(far_out)
+    near_home = exchange(after(near_out, far_home))
+    to_high_2, to_low_3, to_high_3, to_low_4 = combine(far_home, far_mix, [F32, F32, BF16, BF16], True)
+    down, up = along_z(to_low_4, -1), along_z(to_high_3, 1)
+    down, up = along_z(plus(down, to_low_3), -1), along_z(plus(up, to_high_2), 1)
+    near_home = after(near_home, down, up)
+    own, to_low_1, to_high_1, to_low_2 = combine(near_home, near_mix, [F32] * 4, True)
+    down, up = along_z(plus(down, to_low_2), -1), along_z(plus(up, to_high_1), 1)
+    down = along_z(plus(down, to_low_1), -1)
+    return own + up.astype(F32) + down.astype(F32)
 
 
 def solution(mesh):

time: 199 us -> 159 us (0.80)
  starting transfers between devices: 73.7 us -> 38.3 us
  waiting for transfers between devices: 82.4 us -> 57.6 us
  blocking collectives: 0 us -> 24.8 us
  local copies, waits for them, and re-layouts: 14.9 us -> 11.6 us
    ppermute x28 -> x14, starting transfers between devices: 50.8 us -> 22.1 us  [along_z(): lax.ppermute(x, 'expert', [(i, (i + 2 * by) % col_count) for i in range(c...]
    all_to_all x4 -> x3, waiting for transfers between devices: 40.1 us -> 11.9 us  [exchange(): return lax.all_to_all(x, 'dp', split_axis=0, concat_axis=0, tiled=True)]
    all_to_all x0 -> x1, blocking collectives: none -> 24.8 us  [exchange(): return lax.all_to_all(x, 'dp', split_axis=0, concat_axis=0, tiled=True)]
    all_to_all x4 -> x3, starting transfers between devices: 22.3 us -> 15.6 us  [exchange(): return lax.all_to_all(x, 'dp', split_axis=0, concat_axis=0, tiled=True)]
    ppermute x28 -> x14, waiting for transfers between devices: 42.3 us -> 45.7 us  [along_z(): lax.ppermute(x, 'expert', [(i, (i + 2 * by) % col_count) for i in range(c...]
    unnamed x53 -> x31, local copies, waits for them, and re-layouts: 13.7 us -> 10.5 us
  transfers between devices with their start and end apart: 35 -> 20, of which waited for: 18 -> 13; matrix products, arithmetic and copies ran while one was open for 1% -> 0% of each run, Pallas kernels for 10% -> 9%
where the time goes in v3:
time: 159 us; the launch traced here: 158 us
  waiting for transfers between devices  57.6 us (36%)
  starting transfers between devices  38.3 us (24%)
  blocking collectives  24.8 us (16%)
  Pallas kernels  23.4 us (15%)
  local copies, waits for them, and re-layouts  11.6 us (7%)
  other arithmetic  1.87 us (1%)
    ppermute x14, waiting for transfers between devices, along_z(): lax.ppermute(x, 'expert', [(i, (i + 2 * by) % col_count) for i in range(c...  45.7 us
    all_to_all x1, blocking collectives, exchange(): return lax.all_to_all(x, 'dp', split_axis=0, concat_axis=0, tiled=True)  24.8 us
    pallas_call x8, Pallas kernels, kernel_call(): pl.pallas_call(body, out_shape=[pltpu.VMEM(*out) if keep else jax.ShapeDt...  23.4 us
    ppermute x14, starting transfers between devices, along_z(): lax.ppermute(x, 'expert', [(i, (i + 2 * by) % col_count) for i in range(c...  22.1 us
    all_to_all x3, starting transfers between devices, exchange(): return lax.all_to_all(x, 'dp', split_axis=0, concat_axis=0, tiled=True)  15.6 us
    all_to_all x3, waiting for transfers between devices, exchange(): return lax.all_to_all(x, 'dp', split_axis=0, concat_axis=0, tiled=True)  11.9 us
    unnamed x31, local copies, waits for them, and re-layouts  10.5 us
  transfers between devices with their start and end apart: 20, of which 13 were waited for; matrix products, arithmetic and copies ran while one was open for 0% of the time, Pallas kernels for 9%

profile of v3, /device:TPU:96, one launch (start us, length us, event | category | flops | bytes accessed | tf_op | source)
XLA Modules:
  0.0 157.8 jit_solution(7477637873503426201)
XLA Ops:
  2.7 3.2 %collective-permute-start = (bf16[64,2176]{1,0:T(8,128)(2,1)S(1)}, bf16[64,2176]{1,0:T(8,128)(2,1)S(1)}, u32[]{:S(2)}, u32[]{:S(2)}) collective-permute-start(bf16[64,2176]{1,0:T(8,128)(2,1)S(1)} %concatenate.6.refs_0_), channel_id=1, source_target_pairs={{0,2},{1,3},{2,4},{3,5},{4,6},{5,7},{6,8},{7,9},{8,10},{9,11},{10,... | collective-permute-start | bytes 835592 | tf_op jit(solution)/shard_map/ppermute | solution.py:135
  5.9 5.9 %collective-permute-done.refs_1_ = bf16[64,2176]{1,0:T(8,128)(2,1)S(1)} collective-permute-done((bf16[64,2176]{1,0:T(8,128)(2,1)S(1)}, bf16[64,2176]{1,0:T(8,128)(2,1)S(1)}, u32[]{:S(2)}, u32[]{:S(2)}) %collective-permute-start) | collective-permute-done | bytes 278560 | tf_op jit(solution)/shard_map/ppermute | solution.py:135
  11.8 3.7 %collective-permute-start.2 = (bf16[64,2176]{1,0:T(8,128)(2,1)S(1)}, bf16[64,2176]{1,0:T(8,128)(2,1)S(1)}, u32[]{:S(2)}, u32[]{:S(2)}) collective-permute-start(bf16[64,2176]{1,0:T(8,128)(2,1)S(1)} %collective-permute-done.refs_1_), channel_id=1, source_target_pairs={{0,2},{1,3},{2,4},{3,5},{4,6},{5,7},{6,8},{7,9},{8,10},{9,11},{10,... | collective-permute-start | bytes 835592 | tf_op jit(solution)/shard_map/ppermute | solution.py:135
  15.5 5.0 %collective-permute-done.2.refs_3_ = bf16[64,2176]{1,0:T(8,128)(2,1)S(1)} collective-permute-done((bf16[64,2176]{1,0:T(8,128)(2,1)S(1)}, bf16[64,2176]{1,0:T(8,128)(2,1)S(1)}, u32[]{:S(2)}, u32[]{:S(2)}) %collective-permute-start.2) | collective-permute-done | bytes 278560 | tf_op jit(solution)/shard_map/ppermute | solution.py:135
  23.9 7.3 %all-to-all-start = ((bf16[16,24,2048]{2,1,0:T(8,128)(2,1)}), bf16[16,24,2048]{2,1,0:T(8,128)(2,1)}, u32[]{:S(2)}, u32[]{:S(2)}) async-start(bf16[16,24,2048]{2,1,0:T(8,128)(2,1)} %bitcast.24), calls=%async_computation | async-start | bytes 3145728 | tf_op jit(solution)/shard_map/all_to_all | solution.py:154
  31.3 2.5 %collective-permute-start.4 = (bf16[64,2176]{1,0:T(8,128)(2,1)}, bf16[64,2176]{1,0:T(8,128)(2,1)S(1)}, u32[]{:S(2)}, u32[]{:S(2)}) collective-permute-start(bf16[64,2176]{1,0:T(8,128)(2,1)} %copy-done.6), channel_id=1, source_target_pairs={{0,2},{1,3},{2,4},{3,5},{4,6},{5,7},{6,8},{7,9},{8,10},{9,11},{10,... | collective-permute-start | bytes 835592 | tf_op jit(solution)/shard_map/ppermute | solution.py:135
  33.8 4.8 %collective-permute-done.4.refs_1_ = bf16[64,2176]{1,0:T(8,128)(2,1)S(1)} collective-permute-done((bf16[64,2176]{1,0:T(8,128)(2,1)}, bf16[64,2176]{1,0:T(8,128)(2,1)S(1)}, u32[]{:S(2)}, u32[]{:S(2)}) %collective-permute-start.4) | collective-permute-done | bytes 278560 | tf_op jit(solution)/shard_map/ppermute | solution.py:135
  38.6 3.2 %collective-permute-start.6 = (bf16[64,2176]{1,0:T(8,128)(2,1)S(1)}, bf16[64,2176]{1,0:T(8,128)(2,1)S(1)}, u32[]{:S(2)}, u32[]{:S(2)}) collective-permute-start(bf16[64,2176]{1,0:T(8,128)(2,1)S(1)} %collective-permute-done.4.refs_1_), channel_id=1, source_target_pairs={{0,2},{1,3},{2,4},{3,5},{4,6},{5,7},{6,8},{7,9},{8,10},{9,11},{10,... | collective-permute-start | bytes 835592 | tf_op jit(solution)/shard_map/ppermute | solution.py:135
  42.3 3.5 %collective-permute-done.6.refs_3_ = bf16[64,2176]{1,0:T(8,128)(2,1)S(1)} collective-permute-done((bf16[64,2176]{1,0:T(8,128)(2,1)S(1)}, bf16[64,2176]{1,0:T(8,128)(2,1)S(1)}, u32[]{:S(2)}, u32[]{:S(2)}) %collective-permute-start.6) | collective-permute-done | bytes 278560 | tf_op jit(solution)/shard_map/ppermute | solution.py:135
  47.8 5.2 %all-to-all-done = bf16[16,24,2048]{2,1,0:T(8,128)(2,1)} async-done(((bf16[16,24,2048]{2,1,0:T(8,128)(2,1)}), bf16[16,24,2048]{2,1,0:T(8,128)(2,1)}, u32[]{:S(2)}, u32[]{:S(2)}) %all-to-all-start) | async-done | bytes 1572896 | tf_op jit(solution)/shard_map/all_to_all | solution.py:154
  53.1 4.6 %all-to-all-start.1 = ((bf16[16,24,2048]{2,1,0:T(8,128)(2,1)}), bf16[16,24,2048]{2,1,0:T(8,128)(2,1)}, u32[]{:S(2)}, u32[]{:S(2)}) async-start(bf16[16,24,2048]{2,1,0:T(8,128)(2,1)} %bitcast.25), calls=%async_computation.1 | async-start | bytes 3145728 | tf_op jit(solution)/shard_map/all_to_all | solution.py:154
  63.9 9.1 %expert.2 = bf16[384,2048]{1,0:T(8,128)(2,1)} custom-call(bf16[384,2048]{1,0:T(8,128)(2,1)} %bitcast.2.x_ref, bf16[2048,384]{1,0:T(8,128)(2,1)S(1)} %bitcast.13, bf16[2048,384]{1,0:T(8,128)(2,1)} %collective-permute-done.7.g1, bf16[2048,384]{1,0:T(8,128)(2,1)S(1)} %bitcast.16, bf16[2048,384]{1,0:T(8,128)(2,1)} %collective-permute-done.8.u1, ...), custom_call_target="tpu_custom_call" | custom-call | tf_op jit(solution)/shard_map/expert/pallas_call | solution.py:27
  73.0 6.1 %all-to-all-done.1 = bf16[16,24,2048]{2,1,0:T(8,128)(2,1)} async-done(((bf16[16,24,2048]{2,1,0:T(8,128)(2,1)}), bf16[16,24,2048]{2,1,0:T(8,128)(2,1)}, u32[]{:S(2)}, u32[]{:S(2)}) %all-to-all-start.1) | async-done | bytes 1572896 | tf_op jit(solution)/shard_map/all_to_all | solution.py:154
  80.5 7.9 %expert.3 = bf16[384,2048]{1,0:T(8,128)(2,1)S(1)} custom-call(bf16[384,2048]{1,0:T(8,128)(2,1)} %bitcast.7.x_ref, bf16[2048,384]{1,0:T(8,128)(2,1)S(1)} %bitcast.14, bf16[2048,384]{1,0:T(8,128)(2,1)} %collective-permute-done.7.g1, bf16[2048,384]{1,0:T(8,128)(2,1)S(1)} %bitcast.17, bf16[2048,384]{1,0:T(8,128)(2,1)} %collective-permute-done.8.u1, ...), custom_call_target="tpu_custom_call" | custom-call | tf_op jit(solution)/shard_map/expert/pallas_call | solution.py:27
  88.5 24.8 %all_to_all.46 = bf16[16,24,2048]{2,1,0:T(8,128)(2,1)S(1)} all-to-all(bf16[16,24,2048]{2,1,0:T(8,128)(2,1)S(1)} %bitcast.21), channel_id=1, replica_groups=mesh['dp'=16,'expert'=16] {'dp'}, dimensions={0} | all-to-all | bytes 3145728 | tf_op jit(solution)/shard_map/all_to_all | solution.py:154
  113.2 3.7 %all-to-all-start.3 = ((bf16[16,24,2048]{2,1,0:T(8,128)(2,1)}), bf16[16,24,2048]{2,1,0:T(8,128)(2,1)S(1)}, u32[]{:S(2)}, u32[]{:S(2)}) async-start(bf16[16,24,2048]{2,1,0:T(8,128)(2,1)} %bitcast.10), calls=%async_computation.3 | async-start | bytes 3145728 | tf_op jit(solution)/shard_map/all_to_all | solution.py:154
  120.0 2.4 %collective-permute-start.12 = (bf16[64,2048]{1,0:T(8,128)(2,1)S(1)}, bf16[64,2048]{1,0:T(8,128)(2,1)S(1)}, u32[]{:S(2)}, u32[]{:S(2)}) collective-permute-start(bf16[64,2048]{1,0:T(8,128)(2,1)S(1)} %get-tuple-element.42), channel_id=1, source_target_pairs={{0,2},{1,3},{2,4},{3,5},{4,6},{5,7},{6,8},{7,9},{8,10},{9,11},{10,... | collective-permute-start | bytes 786440 | tf_op jit(solution)/shard_map/ppermute | solution.py:135
  122.5 4.3 %collective-permute-done.12 = bf16[64,2048]{1,0:T(8,128)(2,1)S(1)} collective-permute-done((bf16[64,2048]{1,0:T(8,128)(2,1)S(1)}, bf16[64,2048]{1,0:T(8,128)(2,1)S(1)}, u32[]{:S(2)}, u32[]{:S(2)}) %collective-permute-start.12) | collective-permute-done | bytes 262176 | tf_op jit(solution)/shard_map/ppermute | solution.py:135
  126.8 3.6 %collective-permute-start.13 = (bf16[64,2048]{1,0:T(8,128)(2,1)S(1)}, bf16[64,2048]{1,0:T(8,128)(2,1)S(1)}, u32[]{:S(2)}, u32[]{:S(2)}) collective-permute-start(bf16[64,2048]{1,0:T(8,128)(2,1)S(1)} %add_convert_fusion.3), channel_id=1, source_target_pairs={{0,2},{1,3},{2,4},{3,5},{4,6},{5,7},{6,8},{7,9},{8,10},{9,11},{10,... | collective-permute-start | bytes 786440 | tf_op jit(solution)/shard_map/ppermute | solution.py:135
  130.5 3.7 %collective-permute-done.13 = bf16[64,2048]{1,0:T(8,128)(2,1)S(1)} collective-permute-done((bf16[64,2048]{1,0:T(8,128)(2,1)S(1)}, bf16[64,2048]{1,0:T(8,128)(2,1)S(1)}, u32[]{:S(2)}, u32[]{:S(2)}) %collective-permute-start.13) | collective-permute-done | bytes 262176 | tf_op jit(solution)/shard_map/ppermute | solution.py:135
  134.3 3.8 %collective-permute-done.11 = bf16[64,2048]{1,0:T(8,128)(2,1)S(1)} collective-permute-done((bf16[64,2048]{1,0:T(8,128)(2,1)S(1)}, bf16[64,2048]{1,0:T(8,128)(2,1)S(1)}, u32[]{:S(2)}, u32[]{:S(2)}) %collective-permute-start.11) | collective-permute-done | bytes 262176 | tf_op jit(solution)/shard_map/ppermute | solution.py:135
  140.1 3.3 %collective-permute-start.14 = (bf16[64,2048]{1,0:T(8,128)(2,1)S(1)}, bf16[64,2048]{1,0:T(8,128)(2,1)S(1)}, u32[]{:S(2)}, u32[]{:S(2)}) collective-permute-start(bf16[64,2048]{1,0:T(8,128)(2,1)S(1)} %add_convert_fusion.2), channel_id=1, source_target_pairs={{0,2},{1,3},{2,4},{3,5},{4,6},{5,7},{6,8},{7,9},{8,10},{9,11},{10,... | collective-permute-start | bytes 786440 | tf_op jit(solution)/shard_map/ppermute | solution.py:135
  143.4 5.8 %collective-permute-done.15 = bf16[64,2048]{1,0:T(8,128)(2,1)S(1)} collective-permute-done((bf16[64,2048]{1,0:T(8,128)(2,1)S(1)}, bf16[64,2048]{1,0:T(8,128)(2,1)S(1)}, u32[]{:S(2)}, u32[]{:S(2)}) %collective-permute-start.15) | collective-permute-done | bytes 262176 | tf_op jit(solution)/shard_map/ppermute | solution.py:135
  149.4 7.6 %collective-permute-done.16 = bf16[64,2048]{1,0:T(8,128)(2,1)S(1)} collective-permute-done((bf16[64,2048]{1,0:T(8,128)(2,1)S(1)}, bf16[64,2048]{1,0:T(8,128)(2,1)S(1)}, u32[]{:S(2)}, u32[]{:S(2)}) %collective-permute-start.16) | collective-permute-done | bytes 262176 | tf_op jit(solution)/shard_map/ppermute | solution.py:135
  (67 shorter events, 22.7 us)
Async XLA Ops:
  2.7 9.1 %collective-permute-start = (bf16[64,2176]{1,0:T(8,128)(2,1)S(1)}, bf16[64,2176]{1,0:T(8,128)(2,1)S(1)}, u32[]{:S(2)}, u32[]{:S(2)}) collective-permute-start(bf16[64,2176]{1,0:T(8,128)(2,1)S(1)} %concatenate.6.refs_0_), channel_id=1, source_target_pairs={{0,2},{1,3},{2,4},{3,5},{4,6},{5,7},{6,8},{7,9},{8,10},{9,11},{10,... | collective-permute-start | bytes 835592 | tf_op jit(solution)/shard_map/ppermute | solution.py:135
  5.9 9.6 %collective-permute-start.1 = (bf16[64,2176]{1,0:T(8,128)(2,1)S(1)}, bf16[64,2176]{1,0:T(8,128)(2,1)S(1)}, u32[]{:S(2)}, u32[]{:S(2)}) collective-permute-start(bf16[64,2176]{1,0:T(8,128)(2,1)S(1)} %concatenate.6.refs_0_), channel_id=1, source_target_pairs={{0,14},{1,15},{2,0},{3,1},{4,2},{5,3},{6,4},{7,5},{8,6},{9,7},{10,... | collective-permute-start | bytes 835592 | tf_op jit(solution)/shard_map/ppermute | solution.py:135
  11.8 8.7 %collective-permute-start.2 = (bf16[64,2176]{1,0:T(8,128)(2,1)S(1)}, bf16[64,2176]{1,0:T(8,128)(2,1)S(1)}, u32[]{:S(2)}, u32[]{:S(2)}) collective-permute-start(bf16[64,2176]{1,0:T(8,128)(2,1)S(1)} %collective-permute-done.refs_1_), channel_id=1, source_target_pairs={{0,2},{1,3},{2,4},{3,5},{4,6},{5,7},{6,8},{7,9},{8,10},{9,11},{10,... | collective-permute-start | bytes 835592 | tf_op jit(solution)/shard_map/ppermute | solution.py:135
  15.5 8.5 %collective-permute-start.3 = (bf16[64,2176]{1,0:T(8,128)(2,1)S(1)}, bf16[64,2176]{1,0:T(8,128)(2,1)S(1)}, u32[]{:S(2)}, u32[]{:S(2)}) collective-permute-start(bf16[64,2176]{1,0:T(8,128)(2,1)S(1)} %collective-permute-done.1.refs_2_), channel_id=1, source_target_pairs={{0,14},{1,15},{2,0},{3,1},{4,2},{5,3},{6,4},{7,5},{8,6},{9,7},{10,... | collective-permute-start | bytes 835592 | tf_op jit(solution)/shard_map/ppermute | solution.py:135
  23.9 17.8 %copy-start = (bf16[1,2048,384]{2,1,0:T(8,128)(2,1)S(1)}, bf16[1,2048,384]{2,1,0:T(8,128)(2,1)}, u32[]{:S(2)}) copy-start(bf16[1,2048,384]{2,1,0:T(8,128)(2,1)} %param.9) | copy-start | bytes 4718596
  23.9 17.8 %copy-start.1 = (bf16[1,2048,384]{2,1,0:T(8,128)(2,1)S(1)}, bf16[1,2048,384]{2,1,0:T(8,128)(2,1)}, u32[]{:S(2)}) copy-start(bf16[1,2048,384]{2,1,0:T(8,128)(2,1)} %param.10) | copy-start | bytes 4718596
  23.9 29.1 %all-to-all-start = ((bf16[16,24,2048]{2,1,0:T(8,128)(2,1)}), bf16[16,24,2048]{2,1,0:T(8,128)(2,1)}, u32[]{:S(2)}, u32[]{:S(2)}) async-start(bf16[16,24,2048]{2,1,0:T(8,128)(2,1)} %bitcast.24), calls=%async_computation | async-start | bytes 3145728 | tf_op jit(solution)/shard_map/all_to_all | solution.py:154
  31.3 7.3 %collective-permute-start.4 = (bf16[64,2176]{1,0:T(8,128)(2,1)}, bf16[64,2176]{1,0:T(8,128)(2,1)S(1)}, u32[]{:S(2)}, u32[]{:S(2)}) collective-permute-start(bf16[64,2176]{1,0:T(8,128)(2,1)} %copy-done.6), channel_id=1, source_target_pairs={{0,2},{1,3},{2,4},{3,5},{4,6},{5,7},{6,8},{7,9},{8,10},{9,11},{10,... | collective-permute-start | bytes 835592 | tf_op jit(solution)/shard_map/ppermute | solution.py:135
  33.8 8.6 %collective-permute-start.5 = (bf16[64,2176]{1,0:T(8,128)(2,1)S(1)}, bf16[64,2176]{1,0:T(8,128)(2,1)S(1)}, u32[]{:S(2)}, u32[]{:S(2)}) collective-permute-start(bf16[64,2176]{1,0:T(8,128)(2,1)S(1)} %collective-permute-done.3.refs_0_), channel_id=1, source_target_pairs={{0,14},{1,15},{2,0},{3,1},{4,2},{5,3},{6,4},{7,5},{8,6},{9,7},{10,... | collective-permute-start | bytes 835592 | tf_op jit(solution)/shard_map/ppermute | solution.py:135
  38.6 7.2 %collective-permute-start.6 = (bf16[64,2176]{1,0:T(8,128)(2,1)S(1)}, bf16[64,2176]{1,0:T(8,128)(2,1)S(1)}, u32[]{:S(2)}, u32[]{:S(2)}) collective-permute-start(bf16[64,2176]{1,0:T(8,128)(2,1)S(1)} %collective-permute-done.4.refs_1_), channel_id=1, source_target_pairs={{0,2},{1,3},{2,4},{3,5},{4,6},{5,7},{6,8},{7,9},{8,10},{9,11},{10,... | collective-permute-start | bytes 835592 | tf_op jit(solution)/shard_map/ppermute | solution.py:135
  41.7 20.8 %collective-permute-start.7 = (bf16[2048,384]{1,0:T(8,128)(2,1)S(1)}, bf16[2048,384]{1,0:T(8,128)(2,1)}, u32[]{:S(2)}, u32[]{:S(2)}) collective-permute-start(bf16[2048,384]{1,0:T(8,128)(2,1)S(1)} %bitcast.12), channel_id=1, source_target_pairs={{0,1},{1,0},{2,3},{3,2},{4,5},{5,4},{6,7},{7,6},{8,9},{9,8},{10,11... | collective-permute-start | bytes 4718600 | tf_op jit(solution)/shard_map/ppermute | solution.py:140
  41.7 20.8 %collective-permute-start.8 = (bf16[2048,384]{1,0:T(8,128)(2,1)S(1)}, bf16[2048,384]{1,0:T(8,128)(2,1)}, u32[]{:S(2)}, u32[]{:S(2)}) collective-permute-start(bf16[2048,384]{1,0:T(8,128)(2,1)S(1)} %bitcast.15), channel_id=1, source_target_pairs={{0,1},{1,0},{2,3},{3,2},{4,5},{5,4},{6,7},{7,6},{8,9},{9,8},{10,11... | collective-permute-start | bytes 4718600 | tf_op jit(solution)/shard_map/ppermute | solution.py:140
  42.2 20.3 %collective-permute-start.9 = (bf16[384,2048]{1,0:T(8,128)(2,1)}, bf16[384,2048]{1,0:T(8,128)(2,1)}, u32[]{:S(2)}, u32[]{:S(2)}) collective-permute-start(bf16[384,2048]{1,0:T(8,128)(2,1)} %bitcast.18), channel_id=1, source_target_pairs={{0,1},{1,0},{2,3},{3,2},{4,5},{5,4},{6,7},{7,6},{8,9},{9,8},{10,11... | collective-permute-start | bytes 4718600 | tf_op jit(solution)/shard_map/ppermute | solution.py:140
  53.1 26.1 %all-to-all-start.1 = ((bf16[16,24,2048]{2,1,0:T(8,128)(2,1)}), bf16[16,24,2048]{2,1,0:T(8,128)(2,1)}, u32[]{:S(2)}, u32[]{:S(2)}) async-start(bf16[16,24,2048]{2,1,0:T(8,128)(2,1)} %bitcast.25), calls=%async_computation.1 | async-start | bytes 3145728 | tf_op jit(solution)/shard_map/all_to_all | solution.py:154
  113.2 25.4 %all-to-all-start.3 = ((bf16[16,24,2048]{2,1,0:T(8,128)(2,1)}), bf16[16,24,2048]{2,1,0:T(8,128)(2,1)S(1)}, u32[]{:S(2)}, u32[]{:S(2)}) async-start(bf16[16,24,2048]{2,1,0:T(8,128)(2,1)} %bitcast.10), calls=%async_computation.3 | async-start | bytes 3145728 | tf_op jit(solution)/shard_map/all_to_all | solution.py:154
  118.8 19.9 %copy-start.8 = (bf16[256,384]{1,0:T(8,128)(2,1)S(1)}, bf16[256,384]{1,0:T(8,128)(2,1)}, u32[]{:S(2)}) copy-start(bf16[256,384]{1,0:T(8,128)(2,1)} %copy-done.7) | copy-start | bytes 589828
  118.8 19.9 %copy-start.10 = (bf16[256,384]{1,0:T(8,128)(2,1)S(1)}, bf16[256,384]{1,0:T(8,128)(2,1)}, u32[]{:S(2)}) copy-start(bf16[256,384]{1,0:T(8,128)(2,1)} %copy-done.9) | copy-start | bytes 589828
  120.0 6.7 %collective-permute-start.12 = (bf16[64,2048]{1,0:T(8,128)(2,1)S(1)}, bf16[64,2048]{1,0:T(8,128)(2,1)S(1)}, u32[]{:S(2)}, u32[]{:S(2)}) collective-permute-start(bf16[64,2048]{1,0:T(8,128)(2,1)S(1)} %get-tuple-element.42), channel_id=1, source_target_pairs={{0,2},{1,3},{2,4},{3,5},{4,6},{5,7},{6,8},{7,9},{8,10},{9,11},{10,... | collective-permute-start | bytes 786440 | tf_op jit(solution)/shard_map/ppermute | solution.py:135
  122.5 7.9 %collective-permute-start.10 = (bf16[64,2048]{1,0:T(8,128)(2,1)S(1)}, bf16[64,2048]{1,0:T(8,128)(2,1)S(1)}, u32[]{:S(2)}, u32[]{:S(2)}) collective-permute-start(bf16[64,2048]{1,0:T(8,128)(2,1)S(1)} %get-tuple-element.40), channel_id=1, source_target_pairs={{0,14},{1,15},{2,0},{3,1},{4,2},{5,3},{6,4},{7,5},{8,6},{9,7},{10,... | collective-permute-start | bytes 786440 | tf_op jit(solution)/shard_map/ppermute | solution.py:135
  126.8 7.5 %collective-permute-start.13 = (bf16[64,2048]{1,0:T(8,128)(2,1)S(1)}, bf16[64,2048]{1,0:T(8,128)(2,1)S(1)}, u32[]{:S(2)}, u32[]{:S(2)}) collective-permute-start(bf16[64,2048]{1,0:T(8,128)(2,1)S(1)} %add_convert_fusion.3), channel_id=1, source_target_pairs={{0,2},{1,3},{2,4},{3,5},{4,6},{5,7},{6,8},{7,9},{8,10},{9,11},{10,... | collective-permute-start | bytes 786440 | tf_op jit(solution)/shard_map/ppermute | solution.py:135
  130.5 7.7 %collective-permute-start.11 = (bf16[64,2048]{1,0:T(8,128)(2,1)S(1)}, bf16[64,2048]{1,0:T(8,128)(2,1)S(1)}, u32[]{:S(2)}, u32[]{:S(2)}) collective-permute-start(bf16[64,2048]{1,0:T(8,128)(2,1)S(1)} %add_convert_fusion.4), channel_id=1, source_target_pairs={{0,14},{1,15},{2,0},{3,1},{4,2},{5,3},{6,4},{7,5},{8,6},{9,7},{10,... | collective-permute-start | bytes 786440 | tf_op jit(solution)/shard_map/ppermute | solution.py:135
  140.0 9.2 %collective-permute-start.15 = (bf16[64,2048]{1,0:T(8,128)(2,1)S(1)}, bf16[64,2048]{1,0:T(8,128)(2,1)S(1)}, u32[]{:S(2)}, u32[]{:S(2)}) collective-permute-start(bf16[64,2048]{1,0:T(8,128)(2,1)S(1)} %add_convert_fusion.1), channel_id=1, source_target_pairs={{0,14},{1,15},{2,0},{3,1},{4,2},{5,3},{6,4},{7,5},{8,6},{9,7},{10,... | collective-permute-start | bytes 786440 | tf_op jit(solution)/shard_map/ppermute | solution.py:135
  140.1 9.2 %collective-permute-start.14 = (bf16[64,2048]{1,0:T(8,128)(2,1)S(1)}, bf16[64,2048]{1,0:T(8,128)(2,1)S(1)}, u32[]{:S(2)}, u32[]{:S(2)}) collective-permute-start(bf16[64,2048]{1,0:T(8,128)(2,1)S(1)} %add_convert_fusion.2), channel_id=1, source_target_pairs={{0,2},{1,3},{2,4},{3,5},{4,6},{5,7},{6,8},{7,9},{8,10},{9,11},{10,... | collective-permute-start | bytes 786440 | tf_op jit(solution)/shard_map/ppermute | solution.py:135
  149.3 7.7 %collective-permute-start.16 = (bf16[64,2048]{1,0:T(8,128)(2,1)S(1)}, bf16[64,2048]{1,0:T(8,128)(2,1)S(1)}, u32[]{:S(2)}, u32[]{:S(2)}) collective-permute-start(bf16[64,2048]{1,0:T(8,128)(2,1)S(1)} %add_convert_fusion), channel_id=1, source_target_pairs={{0,14},{1,15},{2,0},{3,1},{4,2},{5,3},{6,4},{7,5},{8,6},{9,7},{10,... | collective-permute-start | bytes 786440 | tf_op jit(solution)/shard_map/ppermute | solution.py:135
  (11 other events, 13.1 us)
